TPU v7x, 256 devices: a whole 4x4x8 slice. The times are simulated.
256 devices in a mesh: group: 8 (over x, core), batch: 32 (over z, y).
Axes of the slice: x: 4, y: 4, z: 8, core: 2. Of those that a mesh axis runs over, the one named last changes fastest.
Arguments:
- panel_alleles: int32 [64, 131072], P('group', 'batch'), may hold values 0 or 1
- recomb_rates: float32 [64], P('group'), may hold values from 0.001 to 0.3
- genotypes: int32 [2, 64], P(None, 'group'), may hold values from 0 to 2, as said below
Outputs:
- dosage: float32 [2, 64], P(None, 'group')
- log_likelihood: float32 [2], replicated
Inputs may be any that keep to these rules, and one draw needn't show every extreme that they name: `genotypes`: 2 marks a marker at which the target's allele is missing; 0 and 1 are observed alleles.
All inputs are finite; a program needn't handle non-finite values. No bound on the sum of `panel_alleles` on one device may be relied on, other than what follows from the above.
Results may differ from a plain program's by a relative error of at most 0.0003.
Values sent between devices are 32-bit elements; how exact they have to be, the bound alone decides.
A program may use at most 64 MiB of HBM per device.

v0:
```python
import jax
import jax.numpy as jnp
from jax import lax
from jax.sharding import PartitionSpec as P

K = 131072


MISMATCH = 0.05
HIGHEST = lax.Precision.HIGHEST


def from_behind(x, axis, by):
    peers = lax.axis_size(axis)
    pairs = [(i, i + by) for i in range(peers) if 0 <= i + by < peers]
    return lax.ppermute(x, axis, pairs)


def emission(panel_rows, geno_col):
    observed = geno_col[:, None]
    agrees = jnp.where(panel_rows == observed, 1.0 - MISMATCH, MISMATCH)
    return jnp.where(observed == 2, 1.0, agrees).astype(jnp.float32)


def forward_terms(panel_rows, geno_col, switches):
    emitted = emission(panel_rows, geno_col)
    retain = emitted * (1.0 - switches)[:, None]
    inject = emitted * (switches / K)[:, None]
    return (retain, inject, None)


def backward_terms(panel_rows, geno_col, switches):
    emitted = emission(panel_rows, geno_col)[::-1]
    flipped = switches[::-1]
    retain = emitted * (1.0 - flipped)[:, None]
    inject = jnp.broadcast_to((flipped / K)[:, None], emitted.shape)
    return (retain, inject, emitted)


def partial_sums(entering, retain, inject, weight, extent):
    logs = jnp.cumsum(jnp.log(retain), axis=0)
    shifted = jnp.concatenate([jnp.zeros_like(entering)[None], logs[: extent - 1]], axis=0)
    before = jnp.exp(shifted)
    left_side = before if weight is None else weight * before
    leading = jnp.einsum("jk,k->j", left_side, entering, precision=HIGHEST)
    anchor = shifted[0]
    right_side = inject * jnp.exp(anchor[None] - logs)
    nearby = jnp.exp(jnp.minimum(shifted - anchor[None], 0.0))
    nearby = nearby if weight is None else weight * nearby
    columns = [jnp.einsum("jk,tk->jt", nearby, right_side, precision=HIGHEST)]
    coupling = jnp.concatenate(columns, axis=1)
    return (leading, coupling)


def solve_sums(leading, coupling):
    columns = coupling.shape[1]

    def settle(marker, sigmas):
        below = jnp.arange(columns) < marker
        update = leading[marker] + jnp.sum(
            jnp.where(below, coupling[marker] * sigmas[:columns], 0.0)
        )
        return sigmas.at[marker].set(update)

    return lax.fori_loop(0, leading.shape[0], settle, jnp.zeros_like(leading))


def advance(entering, retain, inject, sigmas, keep_states):

    def advance_single(current, pieces):
        current = pieces[0] * current + pieces[1] * pieces[2]
        return (current, current if keep_states else None)

    return lax.scan(advance_single, entering, (retain, inject, sigmas[: retain.shape[0]]))


def place_rows(store, block, active):
    return jnp.where(active, block, store)


def on_device(panel_alleles, recomb_rates, genotypes):
    chain_size = lax.axis_size("group")
    position = lax.axis_index("group")
    markers, width = panel_alleles.shape
    targets = genotypes.shape[0]
    bundles = targets // targets
    uniform = jnp.full((targets, width), 1.0 / K, jnp.float32)
    first_row = position == 0
    last_row = position == chain_size - 1

    def local_sums(active, arrivals, geno_rows, maker, extent):

        def local_compute():

            def local_single(pieces):
                retain, inject, weight = maker(panel_alleles, pieces[1], recomb_rates)
                return partial_sums(pieces[0], retain, inject, weight, extent)

            return lax.map(local_single, (arrivals, geno_rows))

        def local_skipped():
            return (
                jnp.zeros((targets, extent), jnp.float32),
                jnp.zeros((targets, extent, markers), jnp.float32),
            )

        return lax.cond(active, local_compute, local_skipped)

    def outgoing(active, arrivals, geno_rows, sigmas, maker, scale_row):

        def outgoing_compute():

            def outgoing_single(pieces):
                retain, inject, weight = maker(panel_alleles, pieces[1], recomb_rates)
                ending, unused = advance(pieces[0], retain, inject, pieces[2], False)
                return ending / pieces[2][scale_row]

            return lax.map(outgoing_single, (arrivals, geno_rows, sigmas))

        def outgoing_skipped():
            return jnp.zeros((targets, width), jnp.float32)

        return lax.cond(active, outgoing_compute, outgoing_skipped)

    def moment_step(moment, carried_state):
        (
            sent_forward,
            sent_backward,
            sent_running,
            store_forward,
            store_backward,
            sigma_forward,
            sigma_backward,
            log_terms,
        ) = carried_state
        got_forward = from_behind(sent_forward, "group", 1)
        got_backward = from_behind(sent_backward, "group", -1)
        entering_forward = jnp.where(first_row, uniform, got_forward)
        entering_backward = jnp.where(last_row, uniform, got_backward)
        index_forward = moment - position
        index_backward = moment - (chain_size - 1 - position)
        active_forward = (index_forward >= 0) & (index_forward < bundles)
        active_backward = (index_backward >= 0) & (index_backward < bundles)
        lead_forward, couple_forward = local_sums(
            active_forward, entering_forward, genotypes, forward_terms, markers + 1
        )
        lead_backward, couple_backward = local_sums(
            active_backward, entering_backward, genotypes, backward_terms, markers
        )
        lead_forward, couple_forward, lead_backward, couple_backward = lax.psum(
            (lead_forward, couple_forward, lead_backward, couple_backward), "batch"
        )
        sigmas_forward = jax.vmap(solve_sums)(lead_forward, couple_forward)
        sigmas_backward = jax.vmap(solve_sums)(lead_backward, couple_backward)
        next_forward = outgoing(
            active_forward, entering_forward, genotypes, sigmas_forward, forward_terms, markers
        )
        next_backward = outgoing(
            active_backward,
            entering_backward,
            genotypes,
            sigmas_backward,
            backward_terms,
            markers - 1,
        )
        guarded = jnp.where(active_forward, sigmas_forward[:, markers], 1.0)
        running = jnp.log(guarded)
        store_forward = place_rows(store_forward, entering_forward, active_forward)
        store_backward = place_rows(store_backward, entering_backward, active_backward)
        sigma_forward = place_rows(sigma_forward, sigmas_forward, active_forward)
        sigma_backward = place_rows(sigma_backward, sigmas_backward, active_backward)
        log_terms = place_rows(log_terms, running, active_forward)
        return (
            next_forward,
            next_backward,
            running,
            store_forward,
            store_backward,
            sigma_forward,
            sigma_backward,
            log_terms,
        )

    initial = (
        jnp.zeros((targets, width), jnp.float32),
        jnp.zeros((targets, width), jnp.float32),
        jnp.zeros((targets,), jnp.float32),
        jnp.zeros((targets, width), jnp.float32),
        jnp.zeros((targets, width), jnp.float32),
        jnp.zeros((targets, markers + 1), jnp.float32),
        jnp.zeros((targets, markers), jnp.float32),
        jnp.zeros((targets,), jnp.float32),
    )
    final_state = lax.fori_loop(0, chain_size + bundles - 1, moment_step, initial)
    store_forward, store_backward, sigma_forward, sigma_backward, log_terms = final_state[3:]
    whole_log = lax.psum(log_terms, "group")
    log_likelihood = whole_log / (markers * chain_size)

    def posterior(pieces):
        entering_ahead, entering_behind, geno_col, sigmas_ahead, sigmas_behind = pieces
        retain, inject, weight = forward_terms(panel_alleles, geno_col, recomb_rates)
        unused_f, forward_states = advance(entering_ahead, retain, inject, sigmas_ahead, True)
        forward_rows = forward_states / sigmas_ahead[1:, None]
        retain, inject, weight = backward_terms(panel_alleles, geno_col, recomb_rates)
        unused_b, backward_states = advance(entering_behind, retain, inject, sigmas_behind, True)
        scaled_back = backward_states[:-1] / sigmas_behind[:-1, None]
        backward_rows = jnp.concatenate([entering_behind[None], scaled_back], axis=0)[::-1]
        product = forward_rows * backward_rows
        numerator = jnp.sum(jnp.where(panel_alleles == 1, product, 0.0), axis=1)
        return (numerator, jnp.sum(product, axis=1))

    numerator, denominator = lax.map(
        posterior, (store_forward, store_backward, genotypes, sigma_forward, sigma_backward)
    )
    numerator, denominator = lax.psum((numerator, denominator), "batch")
    return (numerator / denominator, log_likelihood)


def solution(mesh):
    placed = (P("group", "batch"), P("group"), P(None, "group"))
    return jax.shard_map(
        on_device, mesh=mesh, in_specs=placed, out_specs=(P(None, "group"), P()), check_vma=False
    )
```

profile of v0, /device:TPU:1, one launch (start us, length us, event | category | flops | bytes accessed | tf_op | source)
XLA Modules:
  0.0 1798.0 jit_solution(14653522750120755591)
XLA Ops:
  2.0 1592.2 %while.198 = (s32[]{:T(128)}, f32[2,4096]{1,0:T(2,128)}, f32[2,4096]{1,0:T(2,128)}, f32[2,4096]{1,0:T(2,128)S(1)}, f32[2,4096]{1,0:T(2,128)S(1)}, /*index=5*/f32...) while((s32[]{:T(128)}, f32[2,4096]{1,0:T(2,128)}, ...), condition=%wide.region_35.36_spmd.clone, body=%wide.region_0.35_spmd.clone.sunk | while | flops 9048711 | bytes 5607151 | solution.py:194
  14.0 118.2 %all-reduce.5 = (f32[2,9]{1,0:T(2,128)S(1)}, f32[2,9,8]{2,0,1:T(2,128)S(1)}, f32[2,8]{1,0:T(2,128)S(1)}, f32[2,8,8]{2,0,1:T(2,128)S(1)}) all-reduce(f32[2,9]{1,0:T(2,128)} %get-tuple-element.1830, f32[2,9,8]{2,0,1:T(2,128)S(1)} %copy.29, f32[2,8]{1,0:T(2,128)} %get-tuple-element.1833, ...), channel_id=1, replica_groups=mesh['group'=8,'batch'=32] {'batch'}, use_global_device_ids=true, to_apply=%region_6.6 | all-reduce | flops 306 | bytes 2448 | tf_op jit(solution)/shard_map/while/body/eval_jaxpr/psum | solution.py:150
  132.2 17.9 while.201
  167.2 30.1 %collective-permute-start = (f32[2,4096]{1,0:T(2,128)}, f32[2,4096]{1,0:T(2,128)S(1)}, u32[]{:S(2)}, u32[]{:S(2)}) collective-permute-start(f32[2,4096]{1,0:T(2,128)} %get-tuple-element.2213), channel_id=1, source_target_pairs={{0,32},{32,64},{64,96},{96,128},{128,160},{160,192},{192,224},{1,3... | collective-permute-start | bytes 98312 | tf_op jit(solution)/shard_map/while/body/eval_jaxpr/ppermute | solution.py:16
  197.3 28.5 %collective-permute-start.1 = (f32[2,4096]{1,0:T(2,128)}, f32[2,4096]{1,0:T(2,128)S(1)}, u32[]{:S(2)}, u32[]{:S(2)}) collective-permute-start(f32[2,4096]{1,0:T(2,128)} %get-tuple-element.2214), channel_id=1, source_target_pairs={{32,0},{64,32},{96,64},{128,96},{160,128},{192,160},{224,192},{33,... | collective-permute-start | bytes 98312 | tf_op jit(solution)/shard_map/while/body/eval_jaxpr/ppermute | solution.py:16
  234.8 110.5 %all-reduce.5 = (f32[2,9]{1,0:T(2,128)S(1)}, f32[2,9,8]{2,0,1:T(2,128)S(1)}, f32[2,8]{1,0:T(2,128)S(1)}, f32[2,8,8]{2,0,1:T(2,128)S(1)}) all-reduce(f32[2,9]{1,0:T(2,128)} %get-tuple-element.1830, f32[2,9,8]{2,0,1:T(2,128)S(1)} %copy.29, f32[2,8]{1,0:T(2,128)} %get-tuple-element.1833, ...), channel_id=1, replica_groups=mesh['group'=8,'batch'=32] {'batch'}, use_global_device_ids=true, to_apply=%region_6.6 | all-reduce | flops 306 | bytes 2448 | tf_op jit(solution)/shard_map/while/body/eval_jaxpr/psum | solution.py:150
  345.3 17.9 while.201
  379.6 26.4 %conditional.14 = (f32[2,4096]{1,0:T(2,128)}) conditional(s32[]{:T(128)} %convert_element_type.22, () %tuple.344, (f32[2,4096]{1,0:T(2,128)S(1)}, s32[2,8]{1,0:T(2,128)S(1)}, s32[8,4096]{1,0:T(8,128)S(1)}, f32[8]{0:T(128)S(1)}, f32[2,9]{1,0:T(2,128)S(1)}) %tuple.427), branch_computations={%region_12.12_spmd, %region_13.17_spmd} | conditional | flops 245788 | bytes 688914 | solution.py:123
  379.6 26.4 %while.184 = (s32[]{:T(128)}, f32[2,4096]{1,0:T(2,128)}, f32[2,4096]{1,0:T(2,128)S(1)}, s32[2,8]{1,0:T(2,128)S(1)}, s32[8,4096]{1,0:T(8,128)S(1)}, /*index=5*/f3...) while((s32[]{:T(128)}, f32[2,4096]{1,0:T(2,128)}, f32[2,4096]{1,0:T(2,128)S(1)}, ...), condition=%wide.region_17.16_spmd, body=%wide.region_14.15_spmd.sunk | while | flops 245788 | bytes 688818 | solution.py:118
  415.5 110.3 %all-reduce.5 = (f32[2,9]{1,0:T(2,128)S(1)}, f32[2,9,8]{2,0,1:T(2,128)S(1)}, f32[2,8]{1,0:T(2,128)S(1)}, f32[2,8,8]{2,0,1:T(2,128)S(1)}) all-reduce(f32[2,9]{1,0:T(2,128)} %get-tuple-element.1830, f32[2,9,8]{2,0,1:T(2,128)S(1)} %copy.29, f32[2,8]{1,0:T(2,128)} %get-tuple-element.1833, ...), channel_id=1, replica_groups=mesh['group'=8,'batch'=32] {'batch'}, use_global_device_ids=true, to_apply=%region_6.6 | all-reduce | flops 306 | bytes 2448 | tf_op jit(solution)/shard_map/while/body/eval_jaxpr/psum | solution.py:150
  560.8 60.6 %collective-permute-start = (f32[2,4096]{1,0:T(2,128)}, f32[2,4096]{1,0:T(2,128)S(1)}, u32[]{:S(2)}, u32[]{:S(2)}) collective-permute-start(f32[2,4096]{1,0:T(2,128)} %get-tuple-element.2213), channel_id=1, source_target_pairs={{0,32},{32,64},{64,96},{96,128},{128,160},{160,192},{192,224},{1,3... | collective-permute-start | bytes 98312 | tf_op jit(solution)/shard_map/while/body/eval_jaxpr/ppermute | solution.py:16
  628.8 110.7 %all-reduce.5 = (f32[2,9]{1,0:T(2,128)S(1)}, f32[2,9,8]{2,0,1:T(2,128)S(1)}, f32[2,8]{1,0:T(2,128)S(1)}, f32[2,8,8]{2,0,1:T(2,128)S(1)}) all-reduce(f32[2,9]{1,0:T(2,128)} %get-tuple-element.1830, f32[2,9,8]{2,0,1:T(2,128)S(1)} %copy.29, f32[2,8]{1,0:T(2,128)} %get-tuple-element.1833, ...), channel_id=1, replica_groups=mesh['group'=8,'batch'=32] {'batch'}, use_global_device_ids=true, to_apply=%region_6.6 | all-reduce | flops 306 | bytes 2448 | tf_op jit(solution)/shard_map/while/body/eval_jaxpr/psum | solution.py:150
  774.5 29.3 %collective-permute-start = (f32[2,4096]{1,0:T(2,128)}, f32[2,4096]{1,0:T(2,128)S(1)}, u32[]{:S(2)}, u32[]{:S(2)}) collective-permute-start(f32[2,4096]{1,0:T(2,128)} %get-tuple-element.2213), channel_id=1, source_target_pairs={{0,32},{32,64},{64,96},{96,128},{128,160},{160,192},{192,224},{1,3... | collective-permute-start | bytes 98312 | tf_op jit(solution)/shard_map/while/body/eval_jaxpr/ppermute | solution.py:16
  811.7 110.1 %all-reduce.5 = (f32[2,9]{1,0:T(2,128)S(1)}, f32[2,9,8]{2,0,1:T(2,128)S(1)}, f32[2,8]{1,0:T(2,128)S(1)}, f32[2,8,8]{2,0,1:T(2,128)S(1)}) all-reduce(f32[2,9]{1,0:T(2,128)} %get-tuple-element.1830, f32[2,9,8]{2,0,1:T(2,128)S(1)} %copy.29, f32[2,8]{1,0:T(2,128)} %get-tuple-element.1833, ...), channel_id=1, replica_groups=mesh['group'=8,'batch'=32] {'batch'}, use_global_device_ids=true, to_apply=%region_6.6 | all-reduce | flops 306 | bytes 2448 | tf_op jit(solution)/shard_map/while/body/eval_jaxpr/psum | solution.py:150
  956.8 47.8 %collective-permute-start = (f32[2,4096]{1,0:T(2,128)}, f32[2,4096]{1,0:T(2,128)S(1)}, u32[]{:S(2)}, u32[]{:S(2)}) collective-permute-start(f32[2,4096]{1,0:T(2,128)} %get-tuple-element.2213), channel_id=1, source_target_pairs={{0,32},{32,64},{64,96},{96,128},{128,160},{160,192},{192,224},{1,3... | collective-permute-start | bytes 98312 | tf_op jit(solution)/shard_map/while/body/eval_jaxpr/ppermute | solution.py:16
  1020.1 110.2 %all-reduce.5 = (f32[2,9]{1,0:T(2,128)S(1)}, f32[2,9,8]{2,0,1:T(2,128)S(1)}, f32[2,8]{1,0:T(2,128)S(1)}, f32[2,8,8]{2,0,1:T(2,128)S(1)}) all-reduce(f32[2,9]{1,0:T(2,128)} %get-tuple-element.1830, f32[2,9,8]{2,0,1:T(2,128)S(1)} %copy.29, f32[2,8]{1,0:T(2,128)} %get-tuple-element.1833, ...), channel_id=1, replica_groups=mesh['group'=8,'batch'=32] {'batch'}, use_global_device_ids=true, to_apply=%region_6.6 | all-reduce | flops 306 | bytes 2448 | tf_op jit(solution)/shard_map/while/body/eval_jaxpr/psum | solution.py:150
  1165.3 86.8 %collective-permute-start = (f32[2,4096]{1,0:T(2,128)}, f32[2,4096]{1,0:T(2,128)S(1)}, u32[]{:S(2)}, u32[]{:S(2)}) collective-permute-start(f32[2,4096]{1,0:T(2,128)} %get-tuple-element.2213), channel_id=1, source_target_pairs={{0,32},{32,64},{64,96},{96,128},{128,160},{160,192},{192,224},{1,3... | collective-permute-start | bytes 98312 | tf_op jit(solution)/shard_map/while/body/eval_jaxpr/ppermute | solution.py:16
  1265.7 110.3 %all-reduce.5 = (f32[2,9]{1,0:T(2,128)S(1)}, f32[2,9,8]{2,0,1:T(2,128)S(1)}, f32[2,8]{1,0:T(2,128)S(1)}, f32[2,8,8]{2,0,1:T(2,128)S(1)}) all-reduce(f32[2,9]{1,0:T(2,128)} %get-tuple-element.1830, f32[2,9,8]{2,0,1:T(2,128)S(1)} %copy.29, f32[2,8]{1,0:T(2,128)} %get-tuple-element.1833, ...), channel_id=1, replica_groups=mesh['group'=8,'batch'=32] {'batch'}, use_global_device_ids=true, to_apply=%region_6.6 | all-reduce | flops 306 | bytes 2448 | tf_op jit(solution)/shard_map/while/body/eval_jaxpr/psum | solution.py:150
  1409.8 28.6 %conditional.15 = (f32[2,4096]{1,0:T(2,128)}) conditional(s32[]{:T(128)} %convert_element_type.23, () %tuple.351, (f32[2,4096]{1,0:T(2,128)S(1)}, s32[2,8]{1,0:T(2,128)S(1)}, s32[8,4096]{1,0:T(8,128)S(1)}, f32[8]{0:T(128)S(1)}, f32[2,8]{1,0:T(2,128)S(1)}) %tuple.426), branch_computations={%region_29.29_spmd, %region_30.34_spmd} | conditional | flops 147484 | bytes 1147718 | solution.py:123
  1409.8 28.6 %while.188 = (s32[]{:T(128)}, f32[2,4096]{1,0:T(2,128)}, f32[2,4096]{1,0:T(2,128)S(1)}, s32[2,8]{1,0:T(2,128)S(1)}, s32[8,4096]{1,0:T(8,128)S(1)}, /*index=5*/f3...) while((s32[]{:T(128)}, f32[2,4096]{1,0:T(2,128)}, f32[2,4096]{1,0:T(2,128)S(1)}, ...), condition=%wide.region_34.33_spmd, body=%wide.region_31.32_spmd.sunk | while | flops 147484 | bytes 1147622 | solution.py:118
  1448.5 110.6 %all-reduce.5 = (f32[2,9]{1,0:T(2,128)S(1)}, f32[2,9,8]{2,0,1:T(2,128)S(1)}, f32[2,8]{1,0:T(2,128)S(1)}, f32[2,8,8]{2,0,1:T(2,128)S(1)}) all-reduce(f32[2,9]{1,0:T(2,128)} %get-tuple-element.1830, f32[2,9,8]{2,0,1:T(2,128)S(1)} %copy.29, f32[2,8]{1,0:T(2,128)} %get-tuple-element.1833, ...), channel_id=1, replica_groups=mesh['group'=8,'batch'=32] {'batch'}, use_global_device_ids=true, to_apply=%region_6.6 | all-reduce | flops 306 | bytes 2448 | tf_op jit(solution)/shard_map/while/body/eval_jaxpr/psum | solution.py:150
  1594.1 61.6 %while.195 = (s32[]{:T(128)}, f32[2,8]{1,0:T(2,128)S(1)}, f32[2,8]{1,0:T(2,128)S(1)}, s32[8,4096]{1,0:T(8,128)}, f32[2,4096]{1,0:T(2,128)S(1)}, /*index=5*/s32[2...) while((s32[]{:T(128)}, f32[2,8]{1,0:T(2,128)S(1)}, ...), condition=%wide.region_43.44_spmd, body=%wide.region_36.43_spmd.sunk | while | flops 479262 | bytes 3671731 | solution.py:212
  1655.7 55.7 %all-reduce.3 = (f32[2,8]{1,0:T(2,128)S(1)}, f32[2,8]{1,0:T(2,128)S(1)}) all-reduce(f32[2,8]{1,0:T(2,128)S(1)} %get-tuple-element.921, f32[2,8]{1,0:T(2,128)S(1)} %get-tuple-element.922), channel_id=1, replica_groups=mesh['group'=8,'batch'=32] {'batch'}, use_global_device_ids=true, to_apply=%region_44.45 | all-reduce | flops 32 | bytes 256 | tf_op jit(solution)/shard_map/psum | solution.py:215
  1712.0 85.4 %psum.71 = f32[2]{0:T(128)S(1)} all-reduce(f32[2]{0:T(128)S(1)} %get-tuple-element.923), channel_id=1, replica_groups=mesh['group'=8,'batch'=32] {'group'}, use_global_device_ids=true, to_apply=%region_46.47 | all-reduce | flops 2 | bytes 16 | tf_op jit(solution)/shard_map/psum | solution.py:196
  (1819 shorter events, 858.4 us)
Async XLA Ops:
  2.0 6.6 copy-start
  2.0 6.6 collective-permute-start
  6.6 5.4 collective-permute-start.1
  167.2 58.7 %copy-start = (s32[8,4096]{1,0:T(8,128)S(1)}, s32[8,4096]{1,0:T(8,128)}, u32[]{:S(2)}) copy-start(s32[8,4096]{1,0:T(8,128)} %get-tuple-element.2247) | copy-start | bytes 393220 | tf_op jit(solution)/shard_map/while
  167.2 58.6 %collective-permute-start = (f32[2,4096]{1,0:T(2,128)}, f32[2,4096]{1,0:T(2,128)S(1)}, u32[]{:S(2)}, u32[]{:S(2)}) collective-permute-start(f32[2,4096]{1,0:T(2,128)} %get-tuple-element.2213), channel_id=1, source_target_pairs={{0,32},{32,64},{64,96},{96,128},{128,160},{160,192},{192,224},{1,3... | collective-permute-start | bytes 98312 | tf_op jit(solution)/shard_map/while/body/eval_jaxpr/ppermute | solution.py:16
  197.3 35.5 %collective-permute-start.1 = (f32[2,4096]{1,0:T(2,128)}, f32[2,4096]{1,0:T(2,128)S(1)}, u32[]{:S(2)}, u32[]{:S(2)}) collective-permute-start(f32[2,4096]{1,0:T(2,128)} %get-tuple-element.2214), channel_id=1, source_target_pairs={{32,0},{64,32},{96,64},{128,96},{160,128},{192,160},{224,192},{33,... | collective-permute-start | bytes 98312 | tf_op jit(solution)/shard_map/while/body/eval_jaxpr/ppermute | solution.py:16
  406.1 4.5 collective-permute-start
  408.1 5.4 collective-permute-start.1
  560.8 62.6 %copy-start = (s32[8,4096]{1,0:T(8,128)S(1)}, s32[8,4096]{1,0:T(8,128)}, u32[]{:S(2)}) copy-start(s32[8,4096]{1,0:T(8,128)} %get-tuple-element.2247) | copy-start | bytes 393220 | tf_op jit(solution)/shard_map/while
  560.8 62.5 %collective-permute-start = (f32[2,4096]{1,0:T(2,128)}, f32[2,4096]{1,0:T(2,128)S(1)}, u32[]{:S(2)}, u32[]{:S(2)}) collective-permute-start(f32[2,4096]{1,0:T(2,128)} %get-tuple-element.2213), channel_id=1, source_target_pairs={{0,32},{32,64},{64,96},{96,128},{128,160},{160,192},{192,224},{1,3... | collective-permute-start | bytes 98312 | tf_op jit(solution)/shard_map/while/body/eval_jaxpr/ppermute | solution.py:16
  621.4 5.4 collective-permute-start.1
  774.5 31.4 %copy-start = (s32[8,4096]{1,0:T(8,128)S(1)}, s32[8,4096]{1,0:T(8,128)}, u32[]{:S(2)}) copy-start(s32[8,4096]{1,0:T(8,128)} %get-tuple-element.2247) | copy-start | bytes 393220 | tf_op jit(solution)/shard_map/while
  774.5 31.3 %collective-permute-start = (f32[2,4096]{1,0:T(2,128)}, f32[2,4096]{1,0:T(2,128)S(1)}, u32[]{:S(2)}, u32[]{:S(2)}) collective-permute-start(f32[2,4096]{1,0:T(2,128)} %get-tuple-element.2213), channel_id=1, source_target_pairs={{0,32},{32,64},{64,96},{96,128},{128,160},{160,192},{192,224},{1,3... | collective-permute-start | bytes 98312 | tf_op jit(solution)/shard_map/while/body/eval_jaxpr/ppermute | solution.py:16
  803.8 6.0 collective-permute-start.1
  956.8 49.8 %copy-start = (s32[8,4096]{1,0:T(8,128)S(1)}, s32[8,4096]{1,0:T(8,128)}, u32[]{:S(2)}) copy-start(s32[8,4096]{1,0:T(8,128)} %get-tuple-element.2247) | copy-start | bytes 393220 | tf_op jit(solution)/shard_map/while
  956.8 49.7 %collective-permute-start = (f32[2,4096]{1,0:T(2,128)}, f32[2,4096]{1,0:T(2,128)S(1)}, u32[]{:S(2)}, u32[]{:S(2)}) collective-permute-start(f32[2,4096]{1,0:T(2,128)} %get-tuple-element.2213), channel_id=1, source_target_pairs={{0,32},{32,64},{64,96},{96,128},{128,160},{160,192},{192,224},{1,3... | collective-permute-start | bytes 98312 | tf_op jit(solution)/shard_map/while/body/eval_jaxpr/ppermute | solution.py:16
  1004.6 13.5 collective-permute-start.1
  1165.3 88.8 %copy-start = (s32[8,4096]{1,0:T(8,128)S(1)}, s32[8,4096]{1,0:T(8,128)}, u32[]{:S(2)}) copy-start(s32[8,4096]{1,0:T(8,128)} %get-tuple-element.2247) | copy-start | bytes 393220 | tf_op jit(solution)/shard_map/while
  1165.3 88.8 %collective-permute-start = (f32[2,4096]{1,0:T(2,128)}, f32[2,4096]{1,0:T(2,128)S(1)}, u32[]{:S(2)}, u32[]{:S(2)}) collective-permute-start(f32[2,4096]{1,0:T(2,128)} %get-tuple-element.2213), channel_id=1, source_target_pairs={{0,32},{32,64},{64,96},{96,128},{128,160},{160,192},{192,224},{1,3... | collective-permute-start | bytes 98312 | tf_op jit(solution)/shard_map/while/body/eval_jaxpr/ppermute | solution.py:16
  1252.1 5.4 collective-permute-start.1
  1439.1 4.5 collective-permute-start
  1441.1 5.4 collective-permute-start.1
  1610.8 13.9 copy-start.1
  1641.6 13.9 copy-start.1
  (4 other events, 10.5 us)
where the time goes:
time: 1800 us
  blocking collectives  1030 us (57%)
  starting transfers between devices  306 us (17%)
  other arithmetic  271 us (15%)
  local copies, waits for them, and re-layouts  159 us (9%)
  waiting for transfers between devices  18 us (1%)
    psum x8, blocking collectives, moment_step(): lax.psum((lead_forward, couple_forward, lead_backward, couple_backward),...  891 us
    ppermute x16, starting transfers between devices, from_behind(): return lax.ppermute(x, axis, pairs)  306 us
    another operation x280, other arithmetic  185 us
    psum x1, blocking collectives, on_device(): whole_log = lax.psum(log_terms, 'group')  85.4 us
    another operation x472, local copies, waits for them, and re-layouts  62.7 us
    psum x1, blocking collectives, on_device(): numerator, denominator = lax.psum((numerator, denominator), 'batch')  55.7 us
    mul x64, other arithmetic, advance_single(): current = pieces[0] * current + pieces[1] * pieces[2]  41.4 us
    dynamic_slice x64, local copies, waits for them, and re-layouts, advance(): lax.scan(advance_single, entering, (retain, inject, sigmas[:retain.shape[...  40.6 us
  transfers between devices with their start and end apart: 16, of which 7 were waited for; matrix products, arithmetic and copies ran while one was open for 1% of the time, Pallas kernels for 0%

commit v1 on v0

v1 whole, which is shorter than its diff:
```python
import functools
import math

import jax
import jax.numpy as jnp
from jax import lax
from jax.experimental import pallas as pl
from jax.experimental.pallas import tpu as pltpu
from jax.sharding import PartitionSpec as P

HIGHEST = lax.Precision.HIGHEST
MESH = pl.DeviceIdType.MESH

MISMATCH = 0.05
STEP = 0.5 * math.log((1.0 - MISMATCH) / MISMATCH)
LOG_CENTRE = 0.5 * math.log((1.0 - MISMATCH) * MISMATCH)
UP = math.exp(STEP)
DOWN = math.exp(-STEP)
NEG = -1e30
F32 = jnp.float32
BF16 = jnp.bfloat16

MARKERS = 64
BLOCK = 8
BLOCKS = 8


def iota(shape, axis):
    return lax.broadcasted_iota(jnp.int32, shape, axis)


def dot_nt(a, b, precision=None):
    return lax.dot_general(
        a, b, (((1,), (1,)), ((), ())), precision=precision, preferred_element_type=F32
    )


def low_half(x):
    return jnp.where(iota(x.shape, 1) < 64, x, pltpu.roll(x, 64, 1))


def high_half(x):
    return jnp.where(iota(x.shape, 1) < 64, pltpu.roll(x, 64, 1), x)


def meta_tile(rate_row, geno_rows):
    eye = iota((8, 8), 0) == iota((8, 8), 1)
    lane = iota((8, 128), 1)

    def column(row):
        return jnp.sum(jnp.where(eye, jnp.broadcast_to(row, (8, 8)), 0.0), axis=1, keepdims=True)

    rate = column(rate_row)
    first = column(geno_rows[0:1].astype(F32))
    second = column(geno_rows[1:2].astype(F32))
    return jnp.where(lane == 0, rate, jnp.where(lane == 1, first, second))


def anchor_matrix():
    row = iota((128, 64), 0)
    col = iota((128, 64), 1)
    s = row
    t = row - 64
    upper = jnp.where((col >= s) & (col <= 31), 1.0, jnp.where((col >= 32) & (col < s), -1.0, 0.0))
    lower = jnp.where((col >= 32) & (col <= t), 1.0, jnp.where((col > t) & (col <= 31), -1.0, 0.0))
    return jnp.where(row < 64, upper, lower).astype(BF16)


def couplings(signs, genotype):
    width = signs.shape[1]
    sign = jnp.where(genotype == 2.0, 0.0, 2.0 * genotype - 1.0)
    steps = jnp.dot(anchor_matrix(), (signs * sign).astype(BF16), preferred_element_type=F32)
    from_s, to_t = steps[:64], steps[64:]
    u = jnp.exp(STEP * from_s)
    v = jnp.exp(STEP * to_t)
    full = jnp.log(dot_nt(u, jnp.concatenate([v, v], axis=0), HIGHEST))
    left, right = from_s[16:17], to_t[47:48]
    middle = left + right
    top = jnp.max(middle, axis=1, keepdims=True)
    begin = jnp.exp(STEP * (from_s[:16] - left + (middle - top)))
    end = jnp.exp(STEP * (to_t[48:] - right))
    blank = jnp.zeros((48, width), F32)
    corner = jnp.log(dot_nt(begin, jnp.concatenate([blank, end, blank, end], axis=0), HIGHEST))
    corner = corner + STEP * top
    return pack(full, corner)


def pack(full, corner):
    lane = iota((8, 128), 1)
    sub = iota((8, 128), 0)
    col = lane % 64
    rows = [full[8 * a : 8 * a + 8] for a in range(BLOCKS)]
    for a in range(2):
        rows[a] = jnp.where(col >= 48, corner[8 * a : 8 * a + 8], rows[a])
    diagonal = rows[0]
    for a in range(1, BLOCKS):
        diagonal = jnp.where(col // 8 == a, rows[a], diagonal)
    diagonal = jnp.where(col % 8 >= sub, diagonal, 0.0)
    pairs = []
    for a in range(4):
        other = rows[7 - a] if a == 0 else pltpu.roll(rows[7 - a], 8 * a, 1)
        pairs.append(
            jnp.where(col >= 8 * (a + 1), rows[a], jnp.where(col < 8 * a, other, 0.0))
        )
    first = jnp.where(lane < 64, pairs[0], pairs[1])
    second = jnp.where(lane < 64, pairs[2], pairs[3])
    return jnp.concatenate([first, second, diagonal], axis=0)


def unpack(packed):
    first, second, diagonal = packed[0:8], packed[8:16], packed[16:24]
    pairs = [low_half(first), high_half(first), low_half(second), high_half(second)]
    rows = [None] * BLOCKS
    for a in range(4):
        rows[a] = pairs[a]
        rows[7 - a] = pairs[a] if a == 0 else pltpu.roll(pairs[a], 128 - 8 * a, 1)
    col = iota((8, 128), 1) % 64
    return [jnp.where(col // 8 == a, diagonal, rows[a]) for a in range(BLOCKS)], diagonal


def log_total(items):
    top = functools.reduce(jnp.maximum, items)
    return top + jnp.log(functools.reduce(jnp.add, [jnp.exp(x - top) for x in items]))


def row_of(columns):
    col = iota((8, 128), 1) % 64
    sub = iota((8, 128), 0)
    total = None
    for a, column in enumerate(columns):
        part = jnp.where(col == 8 * a + sub, column, 0.0)
        total = part if total is None else total + part
    return jnp.sum(total, axis=0, keepdims=True)


def rate_terms(rates, log_k):
    lane = iota((8, 128), 1)
    col = lane % 64
    sub = iota((8, 128), 0)
    stay = [jnp.log(1.0 - r) for r in rates]
    stay_row = row_of(stay)
    sums = None
    for a in range(BLOCKS):
        part = jnp.where(8 * a + sub <= col, stay[a], 0.0)
        sums = part if sums is None else sums + part
    reach_row = jnp.sum(sums, axis=0, keepdims=True)
    reach_col = [
        jnp.sum(jnp.where((lane < 64) & (col <= 8 * a + sub), stay_row, 0.0), axis=1, keepdims=True)
        for a in range(BLOCKS)
    ]
    jump_col = [jnp.log(r) - log_k for r in rates]
    jump_row = row_of(jump_col)
    start = jnp.full((8, 1), -log_k, F32)
    jump_col[0] = jnp.where(iota((8, 1), 0) == 0, start, jump_col[0])
    return reach_row, reach_col, jump_row, jump_col


def solve(packed, terms, log_k):
    reach_row, reach_col, jump_row, jump_col = terms
    lane = iota((8, 128), 1)
    sub = iota((8, 128), 0)
    col = lane % 64
    block = col // 8
    within = col % 8
    rows, diagonal = unpack(packed)
    paths = [
        jnp.where(col >= 8 * a + sub, rows[a] + (reach_row - reach_col[a]), NEG)
        for a in range(BLOCKS)
    ]
    reach_diag = jnp.broadcast_to(reach_col[0], (8, 128))
    jump_diag = jnp.broadcast_to(jump_col[0], (8, 128))
    for a in range(1, BLOCKS):
        reach_diag = jnp.where(block == a, reach_col[a], reach_diag)
        jump_diag = jnp.where(block == a, jump_col[a], jump_diag)
    path_diag = diagonal + (reach_row - reach_diag)
    ahead = pltpu.roll(path_diag + jump_diag, 7, 0)
    behind = pltpu.roll(path_diag, 1, 1) + jump_row
    inner = jnp.exp(jnp.where(within > sub, jnp.where(lane < 64, ahead, behind), NEG))
    spread = jnp.concatenate(
        [jnp.where(lane % 8 == sub, inner[m : m + 1], 0.0) for m in range(8)], axis=0
    )
    same = (iota((128, 128), 0) // 8 == iota((128, 128), 1) // 8).astype(F32)
    columns = jnp.dot(spread, same, precision=HIGHEST, preferred_element_type=F32)
    inverse = jnp.where(within == sub, 1.0, 0.0)
    for m in range(7):
        inverse = inverse + columns[8 * m : 8 * m + 8] * inverse[m : m + 1]
    forward_inverse = low_half(inverse)
    backward_inverse = high_half(inverse)

    log_sums = []
    injected = []
    reached = jnp.zeros((1, 1), F32)
    for b in range(BLOCKS):
        lead = jnp.exp(paths[b][0:1] + jump_col[b][0:1])
        if b:
            parts = [jnp.exp((injected[a] - reached) + paths[a]) for a in range(b)]
            lead = lead + jnp.sum(functools.reduce(jnp.add, parts), axis=0, keepdims=True)
        sums = jnp.sum(
            jnp.where((block == b) & (lane < 64), lead * forward_inverse, 0.0),
            axis=1,
            keepdims=True,
        )
        here = jnp.broadcast_to(jnp.log(sums) + reached, (8, 128))
        log_sums.append(here)
        injected.append(jump_col[b] + jnp.where(sub == 0, reached, pltpu.roll(here, 1, 0)))
        reached = here[7:8, 0:1]

    row_lane = iota((1, 128), 1)
    row_col = row_lane % 64
    behind_row = jnp.where(row_col == 63, -log_k, NEG)
    back_sums = jnp.zeros((1, 128), F32)
    reached = jnp.zeros((1, 1), F32)
    for b in reversed(range(BLOCKS)):
        lead = jnp.sum(
            jnp.where(lane < 64, jnp.exp(paths[b] + (behind_row - reached)), 0.0),
            axis=1,
            keepdims=True,
        )
        sums = jnp.sum(lead * backward_inverse, axis=0, keepdims=True)
        here = jnp.log(sums) + reached
        back_sums = jnp.where(row_col // 8 == b, here, back_sums)
        if b:
            fresh = pltpu.roll(here + jump_row, 127, 1)
            inside = (row_col >= 8 * b - 1) & (row_col <= 8 * b + 6)
            behind_row = jnp.where(inside, fresh, behind_row)
            reached = here[0:1, 8 * b : 8 * b + 1]
    forward_row = row_of(log_sums)
    return jnp.where(row_lane < 64, forward_row, back_sums)


def by_target(first, second):
    return jnp.where(iota((8, 128), 0) < 4, first, second)


def emission_terms(geno_rows):
    g = by_target(geno_rows[0], geno_rows[1])
    base = jnp.where(g == 2.0, 1.0, jnp.where(g == 1.0, DOWN, UP))
    slope = jnp.where(g == 2.0, 0.0, jnp.where(g == 1.0, UP - DOWN, DOWN - UP))
    return base, slope


def state_terms(solved, rate_row, k):
    lane = iota((8, 128), 1)
    logs = by_target(solved[0], solved[1])
    before = jnp.where(lane == 0, 0.0, pltpu.roll(logs, 1, 1))
    after = jnp.where(lane == 127, 0.0, pltpu.roll(logs, 127, 1))
    over_forward = jnp.exp(before - logs)
    over_backward = pltpu.roll(jnp.exp(after - logs), 64, 1)
    keep = 1.0 - rate_row
    jump = rate_row * (1.0 / k)
    return (
        keep * over_forward,
        jump * over_forward,
        keep * over_backward,
        jnp.broadcast_to(jump, (8, 128)),
    )


def dosage_of(total):
    lane = iota((8, 128), 1)
    sub = iota((8, 128), 0)
    picked = jnp.where((lane // 4) % 2 == sub, total, 0.0)
    src = iota((128, 128), 0)
    dst = iota((128, 128), 1)
    upper = ((src // 8 == dst) & (src < 64)).astype(F32)
    lower = (src // 8 == dst + 8).astype(F32)
    numerator = jnp.dot(picked, upper, precision=HIGHEST, preferred_element_type=F32)
    denominator = jnp.dot(picked, lower, precision=HIGHEST, preferred_element_type=F32)
    return numerator[0:2, 0:8] / denominator[0:2, 0:8]


def kernel(
    n_y, n_z, k,
    panel_ref, rate_ref, geno_ref,
    dosage_ref, like_ref,
    panel_all, meta_all, tiles, emis, fwd, bwd,
    log_send, log_group, log_mid, log_y, log_last, log_z,
    solve_send, solve_recv, sum_send, sum_group, sum_mid, sum_y, sum_last, sum_z,
    own_sem, tile_sem,
    panel_s, panel_r, meta_s, meta_r, group_s, group_r, y_s, y_r, z_s, z_r,
    core_s, core_r, group2_s, group2_r, y2_s, y2_r, z2_s, z2_r,
):
    n_group = BLOCKS
    group = lax.axis_index("group")
    batch = lax.axis_index("batch")
    core = group % 2
    y = batch % n_y
    z = batch // n_y
    width = panel_all.shape[2]
    log_k = math.log(k)

    def in_group(d):
        return (group + d) % n_group

    def group_peer(d):
        return (in_group(d), batch)

    def y_peer(d):
        return (group, z * n_y + (y + d) % n_y)

    def z_peer(d):
        return (group, ((z + d) % n_z) * n_y + y)

    def far_first(n):
        return sorted(range(1, n), key=lambda d: -min(d, n - d))

    barrier = pltpu.get_barrier_semaphore()
    peers = [z_peer(d) for d in far_first(n_z)]
    peers += [group_peer(d) for d in far_first(n_group)]
    peers += [y_peer(d) for d in far_first(n_y)]
    for peer in peers:
        pl.semaphore_signal(barrier, inc=1, device_id=peer, device_id_type=MESH)
    own_panel = pltpu.make_async_copy(
        panel_ref.at[:, pl.ds(pl.multiple_of(group * width, width), width)],
        panel_all.at[group],
        own_sem,
    )
    own_panel.start()
    meta_all[group] = meta_tile(rate_ref[...], geno_ref[...])
    pl.semaphore_wait(barrier, len(peers))

    def remote(src, dst, send, recv, peer):
        return pltpu.make_async_remote_copy(
            src_ref=src, dst_ref=dst, send_sem=send, recv_sem=recv,
            device_id=peer, device_id_type=MESH,
        )

    copies = []
    for d in far_first(n_group):
        start = pl.multiple_of(in_group(d) * width, width)
        copies.append(
            remote(
                panel_ref.at[:, pl.ds(start, width)], panel_all.at[group],
                panel_s.at[d - 1], panel_r.at[d - 1], group_peer(d),
            )
        )
        copies.append(
            remote(
                meta_all.at[group], meta_all.at[group],
                meta_s.at[d - 1], meta_r.at[d - 1], group_peer(d),
            )
        )
    for copy in copies:
        copy.start()
    own_panel.wait()
    for copy in copies:
        copy.wait()

    relayout = []
    for c in range(4):
        for h in range(2):
            copy = pltpu.make_async_copy(
                panel_all.at[:, :, pl.ds(128 * c, 128)],
                tiles.at[:, :, 4 * h + c],
                tile_sem.at[4 * h + c],
            )
            copy.start()
            relayout.append(copy)

    meta = meta_all[...].reshape(MARKERS, 128)
    signs = 2.0 * panel_all[...].reshape(MARKERS, width).astype(F32) - 1.0
    for h in range(2):
        log_send[h] = couplings(signs, meta[:, 1 + h : 2 + h])

    def start_all(n, order, src, slots, send, recv, peer):
        out = [
            remote(src(d), slots.at[d - 1], send.at[d - 1], recv.at[d - 1], peer(d)) for d in order
        ]
        for copy in out:
            copy.start()
        return out

    def finish(copies):
        for copy in copies:
            copy.wait()

    flying = start_all(
        n_group, far_first(n_group), lambda d: log_send.at[in_group(d) % 2],
        log_group, group_s, group_r, group_peer,
    )
    rates = [meta[8 * a : 8 * a + 8, 0:1] for a in range(BLOCKS)]
    terms = rate_terms(rates, log_k)
    rate_row = row_of(rates)
    geno_rows = [
        row_of([meta[8 * a : 8 * a + 8, 1 + h : 2 + h] for a in range(BLOCKS)]) for h in range(2)
    ]
    finish(flying)
    total = log_total([log_send[core]] + [log_group[d] for d in range(n_group - 1)])
    if n_y > 1:
        log_mid[...] = total
        flying = start_all(
            n_y, far_first(n_y), lambda d: log_mid, log_y, y_s, y_r, y_peer
        )
        finish(relayout)
        finish(flying)
        total = log_total([total] + [log_y[d] for d in range(n_y - 1)])
    else:
        finish(relayout)
    base, slope = emission_terms(geno_rows)

    def emissions():
        for t in range(MARKERS):
            allele = tiles[t // 8, t % 8].astype(F32)
            emis[t] = base[:, t : t + 1] + slope[:, t : t + 1] * allele

    if n_z > 1:
        log_last[...] = total
        flying = start_all(
            n_z, far_first(n_z), lambda d: log_last, log_z, z_s, z_r, z_peer
        )
        emissions()
        finish(flying)
        total = log_total([total] + [log_z[d] for d in range(n_z - 1)])
    else:
        emissions()

    mine = solve(total, terms, log_k)
    solve_send[...] = mine
    partner = (group + 1 - 2 * core, batch)
    swap = remote(solve_send, solve_recv, core_s, core_r, partner)
    swap.start()
    swap.wait()
    theirs = solve_recv[...]
    solved = [jnp.where(core == 0, mine, theirs), jnp.where(core == 0, theirs, mine)]

    lane_row = iota((1, 128), 1)
    likes = []
    for h in range(2):
        seen = jnp.sum(
            jnp.where((lane_row < 64) & (geno_rows[h] != 2.0), LOG_CENTRE, 0.0),
            axis=1, keepdims=True,
        )
        likes.append((solved[h][:, 63:64] + seen) * (1.0 / MARKERS))
    like_ref[...] = jnp.where(lane_row == 0, likes[0], likes[1])[:, 0:2]

    keep_f, jump_f, keep_b, jump_b = state_terms(solved, rate_row, float(k))
    ahead = jnp.full((8, 128), 1.0 / k, F32)
    behind = jnp.full((8, 128), 1.0 / k, F32)
    for i in range(MARKERS):
        ahead = emis[i] * (keep_f[:, i : i + 1] * ahead + jump_f[:, i : i + 1])
        fwd[i] = ahead
        t = MARKERS - 1 - i
        bwd[t] = behind
        behind = keep_b[:, t : t + 1] * (emis[t] * behind) + jump_b[:, t : t + 1]

    ones = jnp.ones((8, 128), BF16)
    for a in range(BLOCKS):
        both = fwd[8 * a : 8 * a + 8] * bwd[8 * a : 8 * a + 8]
        carrying = both * tiles[a].astype(F32)
        stacked = jnp.concatenate([carrying.reshape(64, 128), both.reshape(64, 128)], axis=0)
        coarse = stacked.astype(BF16)
        fine = (stacked - coarse.astype(F32)).astype(BF16)
        sums = dot_nt(ones, coarse) + dot_nt(ones, fine)
        sum_send[a] = sums[0:1]

    flying = start_all(
        n_group, far_first(n_group), lambda d: sum_send.at[in_group(d)],
        sum_group, group2_s, group2_r, group_peer,
    )
    finish(flying)
    total = functools.reduce(
        jnp.add, [sum_send[group]] + [sum_group[d] for d in range(n_group - 1)]
    )
    if n_y > 1:
        sum_mid[...] = total
        flying = start_all(
            n_y, far_first(n_y), lambda d: sum_mid, sum_y, y2_s, y2_r, y_peer
        )
        finish(flying)
        total = functools.reduce(jnp.add, [total] + [sum_y[d] for d in range(n_y - 1)])
    if n_z > 1:
        sum_last[...] = total
        flying = start_all(
            n_z, far_first(n_z), lambda d: sum_last, sum_z, z2_s, z2_r, z_peer
        )
        finish(flying)
        total = functools.reduce(jnp.add, [total] + [sum_z[d] for d in range(n_z - 1)])
    dosage_ref[...] = dosage_of(total)


def on_device(n_y, panel, rates, genotypes):
    n_batch = lax.axis_size("batch")
    n_group = lax.axis_size("group")
    n_z = n_batch // n_y
    width = panel.shape[1] // n_group
    k = panel.shape[1] * n_batch
    dma = pltpu.SemaphoreType.DMA
    vmem = pltpu.VMEM
    g1, y1, z1 = n_group - 1, max(n_y - 1, 1), max(n_z - 1, 1)
    scratch = [
        vmem((BLOCKS, BLOCK, width), jnp.int32),
        vmem((BLOCKS, BLOCK, 128), F32),
        vmem((BLOCKS, BLOCK, 8, 128), jnp.int32),
        vmem((MARKERS, 8, 128), F32),
        vmem((MARKERS, 8, 128), F32),
        vmem((MARKERS, 8, 128), F32),
        vmem((2, 24, 128), F32),
        vmem((g1, 24, 128), F32),
        vmem((24, 128), F32),
        vmem((y1, 24, 128), F32),
        vmem((24, 128), F32),
        vmem((z1, 24, 128), F32),
        vmem((1, 128), F32),
        vmem((1, 128), F32),
        vmem((BLOCKS, 1, 128), F32),
        vmem((g1, 1, 128), F32),
        vmem((1, 128), F32),
        vmem((y1, 1, 128), F32),
        vmem((1, 128), F32),
        vmem((z1, 1, 128), F32),
        dma,
        dma((8,)),
        dma((g1,)), dma((g1,)), dma((g1,)), dma((g1,)), dma((g1,)), dma((g1,)),
        dma((y1,)), dma((y1,)), dma((z1,)), dma((z1,)),
        dma, dma,
        dma((g1,)), dma((g1,)), dma((y1,)), dma((y1,)), dma((z1,)), dma((z1,)),
    ]
    dosage, like = pl.pallas_call(
        functools.partial(kernel, n_y, n_z, k),
        out_shape=(
            jax.ShapeDtypeStruct((2, BLOCK), F32),
            jax.ShapeDtypeStruct((1, 2), F32),
        ),
        in_specs=[
            pl.BlockSpec(memory_space=pl.ANY),
            pl.BlockSpec(memory_space=pltpu.VMEM),
            pl.BlockSpec(memory_space=pltpu.VMEM),
        ],
        out_specs=(
            pl.BlockSpec(memory_space=pltpu.VMEM),
            pl.BlockSpec(memory_space=pltpu.VMEM),
        ),
        scratch_shapes=scratch,
        compiler_params=pltpu.CompilerParams(collective_id=0, has_side_effects=True),
    )(panel, rates.reshape(1, BLOCK), genotypes)
    return dosage, like.reshape(2)


def solution(mesh, n_y=4):
    placed = (P("group", "batch"), P("group"), P(None, "group"))
    return jax.shard_map(
        functools.partial(on_device, n_y),
        mesh=mesh,
        in_specs=placed,
        out_specs=(P(None, "group"), P()),
        check_vma=False,
    )
```

time: 1800 us -> 45.7 us (0.03)
  blocking collectives: 1030 us -> 0 us
  starting transfers between devices: 306 us -> 0 us
  other arithmetic: 271 us -> 0 us
  local copies, waits for them, and re-layouts: 159 us -> 1.8 us
  Pallas kernels: 0 us -> 43 us
  waiting for transfers between devices: 18 us -> 0 us
    psum x10 -> x0, blocking collectives: 1030 us -> none  [the longest x8 891 us: moment_step(): lax.psum((lead_forward, couple_forward, lead_backward, couple_backward),...]
    ppermute x16 -> x0, starting transfers between devices: 306 us -> none  [from_behind(): return lax.ppermute(x, axis, pairs)]
    another operation x284 -> x0, other arithmetic: 186 us -> none
    another operation x472 -> x0, local copies, waits for them, and re-layouts: 62.7 us -> none
    mul x76 -> x0, other arithmetic: 44.2 us -> none  [the longest x64 41.4 us: advance_single(): current = pieces[0] * current + pieces[1] * pieces[2]]
    pallas_call x0 -> x1, Pallas kernels: none -> 43 us  [on_device(): pl.pallas_call(functools.partial(kernel, n_y, n_z, k), out_shape=(jax.Sha...]
    dynamic_slice x78 -> x0, local copies, waits for them, and re-layouts: 40.9 us -> none  [the longest x64 40.6 us: advance(): lax.scan(advance_single, entering, (retain, inject, sigmas[:retain.shape[...]
    dynamic_update_slice x44 -> x0, local copies, waits for them, and re-layouts: 23.6 us -> none  [the longest x32 12.5 us: advance(): lax.scan(advance_single, entering, (retain, inject, sigmas[:retain.shape[...]
  transfers between devices with their start and end apart: 16 -> 0, of which waited for: 7 -> 0; matrix products, arithmetic and copies ran while one was open for 1% -> 0% of each run, Pallas kernels for 0% -> 0%
where the time goes in v1:
time: 45.7 us; the launch traced here: 45.4 us
  Pallas kernels  43 us (94%)
  local copies, waits for them, and re-layouts  1.8 us (4%)
  between operations  0.65 us (1%)
    pallas_call x1, Pallas kernels, on_device(): pl.pallas_call(functools.partial(kernel, n_y, n_z, k), out_shape=(jax.Sha...  43 us
    unnamed x6, local copies, waits for them, and re-layouts  1.8 us

profile of v1, /device:TPU:1, one launch (start us, length us, event | category | flops | bytes accessed | tf_op | source)
XLA Modules:
  0.0 45.4 jit_solution(13840905200236665110)
XLA Ops:
  0.6 43.0 %shard_map.50 = (f32[2,8]{1,0:T(2,128)}, f32[1,2]{1,0:T(1,128)}) custom-call(s32[8,4096]{1,0:T(8,128)} %panel_ref.1, f32[1,8]{1,0:T(1,128)} %bitcast.2, s32[2,8]{1,0:T(2,128)} %geno_ref.1), custom_call_target="tpu_custom_call" | custom-call | tf_op jit(solution)/shard_map/pallas_call | solution.py:518
  43.6 0.0 copy-start
  43.6 0.7 %copy-done = f32[2,8]{1,0:T(2,128)S(1)} copy-done((f32[2,8]{1,0:T(2,128)S(1)}, f32[2,8]{1,0:T(2,128)}, u32[]{:S(2)}) %copy-start) | copy-done | bytes 88
  44.3 0.0 copy-start.1
  44.3 0.6 %copy.7 = f32[2,8]{1,0:T(2,128)} copy(f32[2,8]{1,0:T(2,128)S(1)} %copy-done) | data formatting | bytes 128
  44.8 0.1 copy-done.1
  44.9 0.5 %copy.8 = f32[2]{0:T(128)} copy(f32[2]{0:T(128)S(1)} %bitcast.3) | data formatting | bytes 16
Async XLA Ops:
  43.6 0.7 %copy-start = (f32[2,8]{1,0:T(2,128)S(1)}, f32[2,8]{1,0:T(2,128)}, u32[]{:S(2)}) copy-start(f32[2,8]{1,0:T(2,128)} %get-tuple-element.8) | copy-start | bytes 196
  44.3 0.6 %copy-start.1 = (f32[1,2]{1,0:T(1,128)S(1)}, f32[1,2]{1,0:T(1,128)}, u32[]{:S(2)}) copy-start(f32[1,2]{1,0:T(1,128)} %get-tuple-element.5) | copy-start | bytes 28

commit v2 on v1

--- a/solution.py
+++ b/solution.py
@@ -275,10 +275,10 @@
     dosage_ref, like_ref,
     panel_all, meta_all, tiles, emis, fwd, bwd,
     log_send, log_group, log_mid, log_y, log_last, log_z,
-    solve_send, solve_recv, sum_send, sum_group, sum_mid, sum_y, sum_last, sum_z,
+    solve_send, solve_recv, sum_send, sum_group, sum_mid, sum_batch,
     own_sem, tile_sem,
     panel_s, panel_r, meta_s, meta_r, group_s, group_r, y_s, y_r, z_s, z_r,
-    core_s, core_r, group2_s, group2_r, y2_s, y2_r, z2_s, z2_r,
+    core_s, core_r, group2_s, group2_r, batch_s, batch_r,
 ):
     n_group = BLOCKS
     group = lax.axis_index("group")
@@ -305,8 +305,8 @@
         return sorted(range(1, n), key=lambda d: -min(d, n - d))
 
     barrier = pltpu.get_barrier_semaphore()
-    peers = [z_peer(d) for d in far_first(n_z)]
-    peers += [group_peer(d) for d in far_first(n_group)]
+    peers = [group_peer(d) for d in far_first(n_group)]
+    peers += [z_peer(d) for d in far_first(n_z)]
     peers += [y_peer(d) for d in far_first(n_y)]
     for peer in peers:
         pl.semaphore_signal(barrier, inc=1, device_id=peer, device_id_type=MESH)
@@ -391,14 +391,12 @@
         flying = start_all(
             n_y, far_first(n_y), lambda d: log_mid, log_y, y_s, y_r, y_peer
         )
-        finish(relayout)
         finish(flying)
         total = log_total([total] + [log_y[d] for d in range(n_y - 1)])
-    else:
+    base, slope = emission_terms(geno_rows)
+
+    def emissions():
         finish(relayout)
-    base, slope = emission_terms(geno_rows)
-
-    def emissions():
         for t in range(MARKERS):
             allele = tiles[t // 8, t % 8].astype(F32)
             emis[t] = base[:, t : t + 1] + slope[:, t : t + 1] * allele
@@ -461,20 +459,20 @@
     total = functools.reduce(
         jnp.add, [sum_send[group]] + [sum_group[d] for d in range(n_group - 1)]
     )
-    if n_y > 1:
-        sum_mid[...] = total
-        flying = start_all(
-            n_y, far_first(n_y), lambda d: sum_mid, sum_y, y2_s, y2_r, y_peer
-        )
-        finish(flying)
-        total = functools.reduce(jnp.add, [total] + [sum_y[d] for d in range(n_y - 1)])
-    if n_z > 1:
-        sum_last[...] = total
-        flying = start_all(
-            n_z, far_first(n_z), lambda d: sum_last, sum_z, z2_s, z2_r, z_peer
-        )
-        finish(flying)
-        total = functools.reduce(jnp.add, [total] + [sum_z[d] for d in range(n_z - 1)])
+    n_batch = n_y * n_z
+    sum_mid[...] = total
+    flying = [
+        remote(
+            sum_mid, sum_batch.at[pl.ds(d - 1, 1)], batch_s.at[d - 1], batch_r.at[d - 1],
+            (group, (batch + d) % n_batch),
+        )
+        for d in range(1, n_batch)
+    ]
+    for copy in flying:
+        copy.start()
+    sum_batch[n_batch - 1 : n_batch] = total
+    finish(flying)
+    total = jnp.sum(sum_batch[...], axis=0, keepdims=True)
     dosage_ref[...] = dosage_of(total)
 
 
@@ -505,15 +503,13 @@
         vmem((BLOCKS, 1, 128), F32),
         vmem((g1, 1, 128), F32),
         vmem((1, 128), F32),
-        vmem((y1, 1, 128), F32),
-        vmem((1, 128), F32),
-        vmem((z1, 1, 128), F32),
+        vmem((n_batch, 128), F32),
         dma,
         dma((8,)),
         dma((g1,)), dma((g1,)), dma((g1,)), dma((g1,)), dma((g1,)), dma((g1,)),
         dma((y1,)), dma((y1,)), dma((z1,)), dma((z1,)),
         dma, dma,
-        dma((g1,)), dma((g1,)), dma((y1,)), dma((y1,)), dma((z1,)), dma((z1,)),
+        dma((g1,)), dma((g1,)), dma((n_batch - 1,)), dma((n_batch - 1,)),
     ]
     dosage, like = pl.pallas_call(
         functools.partial(kernel, n_y, n_z, k),

time: 45.7 us -> 44.8 us (0.980)
  Pallas kernels: 43 us -> 42.2 us
    pallas_call x1, Pallas kernels: 43 us -> 42.2 us  [on_device(): pl.pallas_call(functools.partial(kernel, n_y, n_z, k), out_shape=(jax.Sha...]
where the time goes in v2:
time: 44.8 us; the launch traced here: 44.7 us
  Pallas kernels  42.2 us (94%)
  local copies, waits for them, and re-layouts  1.8 us (4%)
  between operations  0.65 us (1%)
    pallas_call x1, Pallas kernels, on_device(): pl.pallas_call(functools.partial(kernel, n_y, n_z, k), out_shape=(jax.Sha...  42.2 us
    unnamed x6, local copies, waits for them, and re-layouts  1.8 us

profile of v2, /device:TPU:1, one launch (start us, length us, event | category | flops | bytes accessed | tf_op | source)
XLA Modules:
  0.0 44.7 jit_solution(10650700110780572762)
XLA Ops:
  0.6 42.2 %shard_map.50 = (f32[2,8]{1,0:T(2,128)}, f32[1,2]{1,0:T(1,128)}) custom-call(s32[8,4096]{1,0:T(8,128)} %panel_ref.1, f32[1,8]{1,0:T(1,128)} %bitcast.2, s32[2,8]{1,0:T(2,128)} %geno_ref.1), custom_call_target="tpu_custom_call" | custom-call | tf_op jit(solution)/shard_map/pallas_call | solution.py:514
  42.9 0.0 copy-start
  42.9 0.7 %copy-done = f32[2,8]{1,0:T(2,128)S(1)} copy-done((f32[2,8]{1,0:T(2,128)S(1)}, f32[2,8]{1,0:T(2,128)}, u32[]{:S(2)}) %copy-start) | copy-done | bytes 88
  43.5 0.0 copy-start.1
  43.5 0.6 %copy.7 = f32[2,8]{1,0:T(2,128)} copy(f32[2,8]{1,0:T(2,128)S(1)} %copy-done) | data formatting | bytes 128
  44.1 0.1 copy-done.1
  44.2 0.5 %copy.8 = f32[2]{0:T(128)} copy(f32[2]{0:T(128)S(1)} %bitcast.3) | data formatting | bytes 16
Async XLA Ops:
  42.9 0.7 %copy-start = (f32[2,8]{1,0:T(2,128)S(1)}, f32[2,8]{1,0:T(2,128)}, u32[]{:S(2)}) copy-start(f32[2,8]{1,0:T(2,128)} %get-tuple-element.8) | copy-start | bytes 196
  43.5 0.6 %copy-start.1 = (f32[1,2]{1,0:T(1,128)S(1)}, f32[1,2]{1,0:T(1,128)}, u32[]{:S(2)}) copy-start(f32[1,2]{1,0:T(1,128)} %get-tuple-element.5) | copy-start | bytes 28

commit v3 on v2

--- a/solution.py
+++ b/solution.py
@@ -179,52 +179,83 @@
     spread = jnp.concatenate(
         [jnp.where(lane % 8 == sub, inner[m : m + 1], 0.0) for m in range(8)], axis=0
     )
-    same = (iota((128, 128), 0) // 8 == iota((128, 128), 1) // 8).astype(F32)
-    columns = jnp.dot(spread, same, precision=HIGHEST, preferred_element_type=F32)
+    same = (iota((128, 128), 0) // 8 == iota((128, 128), 1) // 8).astype(BF16)
+    coarse = spread.astype(BF16)
+    fine = (spread - coarse.astype(F32)).astype(BF16)
+    columns = jnp.dot(coarse, same, preferred_element_type=F32)
+    columns = columns + jnp.dot(fine, same, preferred_element_type=F32)
     inverse = jnp.where(within == sub, 1.0, 0.0)
     for m in range(7):
         inverse = inverse + columns[8 * m : 8 * m + 8] * inverse[m : m + 1]
-    forward_inverse = low_half(inverse)
+    forward_inverse = jnp.where(lane < 64, inverse, 0.0)
     backward_inverse = high_half(inverse)
 
-    log_sums = []
-    injected = []
-    reached = jnp.zeros((1, 1), F32)
-    for b in range(BLOCKS):
-        lead = jnp.exp(paths[b][0:1] + jump_col[b][0:1])
-        if b:
-            parts = [jnp.exp((injected[a] - reached) + paths[a]) for a in range(b)]
-            lead = lead + jnp.sum(functools.reduce(jnp.add, parts), axis=0, keepdims=True)
-        sums = jnp.sum(
-            jnp.where((block == b) & (lane < 64), lead * forward_inverse, 0.0),
-            axis=1,
-            keepdims=True,
-        )
-        here = jnp.broadcast_to(jnp.log(sums) + reached, (8, 128))
-        log_sums.append(here)
-        injected.append(jump_col[b] + jnp.where(sub == 0, reached, pltpu.roll(here, 1, 0)))
-        reached = here[7:8, 0:1]
+    offset = jnp.broadcast_to(paths[0][7:8], (8, 128))
+    for a in range(1, BLOCKS):
+        offset = jnp.where(sub == a, paths[a][7:8], offset)
+    offset = jnp.where((within == 0) & (block > sub), offset, 0.0)
+    for step in (1, 2, 4):
+        offset = offset + pltpu.roll(offset, step, 1)
+    factors = [jnp.exp(paths[a] - offset[a : a + 1]) for a in range(BLOCKS)]
+    jumps = [jnp.broadcast_to(jnp.exp(j), (8, 128)) for j in jump_col]
+    jumps_row = jnp.exp(jump_row)
 
     row_lane = iota((1, 128), 1)
     row_col = row_lane % 64
-    behind_row = jnp.where(row_col == 63, -log_k, NEG)
-    back_sums = jnp.zeros((1, 128), F32)
-    reached = jnp.zeros((1, 1), F32)
-    for b in reversed(range(BLOCKS)):
-        lead = jnp.sum(
-            jnp.where(lane < 64, jnp.exp(paths[b] + (behind_row - reached)), 0.0),
-            axis=1,
-            keepdims=True,
-        )
-        sums = jnp.sum(lead * backward_inverse, axis=0, keepdims=True)
-        here = jnp.log(sums) + reached
-        back_sums = jnp.where(row_col // 8 == b, here, back_sums)
+    zero = jnp.zeros((1, 128), F32)
+
+    sums = []
+    scales = [zero, zero]
+    last = jnp.ones((1, 128), F32)
+    spent = jnp.zeros((8, 128), F32)
+    scale_col = jnp.zeros((8, 128), F32)
+
+    back = zero
+    back_scales = [zero, zero]
+    back_scale_row = zero
+    back_sums = zero
+    behind_row = jnp.where(row_lane == 63, math.exp(-log_k), 0.0)
+
+    for b in range(BLOCKS):
+        entering = last * jumps[b][0:1]
+        lead = entering * factors[b][0:1]
         if b:
-            fresh = pltpu.roll(here + jump_row, 127, 1)
-            inside = (row_col >= 8 * b - 1) & (row_col <= 8 * b + 6)
+            weight = jnp.where(sub < b, jnp.exp(offset + scale_col - scales[b]), 0.0)
+            lead = lead + jnp.sum(weight * spent, axis=0, keepdims=True)
+        here = jnp.sum(
+            jnp.where(block == b, lead * forward_inverse, 0.0), axis=1, keepdims=True
+        )
+        here = jnp.broadcast_to(here, (8, 128))
+        sums.append(here)
+        injected = jumps[b] * jnp.where(sub == 0, last, pltpu.roll(here, 1, 0))
+        if b < BLOCKS - 1:
+            spent = jnp.where(
+                sub == b, jnp.sum(injected * factors[b], axis=0, keepdims=True), spent
+            )
+            scale_col = jnp.where(sub == b, scales[b], scale_col)
+            last = here[7:8] * jnp.exp(scales[b] - scales[b + 1])
+            scales.append(jnp.log(here[7:8]) + scales[b])
+
+        c = BLOCKS - 1 - b
+        weight = jnp.exp(offset[c : c + 1] + back_scale_row - back_scales[b])
+        weight = jnp.where((row_lane >= 8 * c + 7) & (row_lane < 64), weight * behind_row, 0.0)
+        lead = jnp.sum(factors[c] * weight, axis=1, keepdims=True)
+        back = jnp.sum(lead * backward_inverse, axis=0, keepdims=True)
+        back_sums = jnp.where(row_col // 8 == c, jnp.log(back) + back_scales[b], back_sums)
+        if c:
+            fresh = pltpu.roll(back * jumps_row, 127, 1)
+            inside = (row_lane >= 8 * c - 1) & (row_lane <= 8 * c + 6)
             behind_row = jnp.where(inside, fresh, behind_row)
-            reached = here[0:1, 8 * b : 8 * b + 1]
-    forward_row = row_of(log_sums)
+            back_scale_row = jnp.where(inside, back_scales[b], back_scale_row)
+            first = jnp.sum(
+                jnp.where(row_lane == 8 * c, back, 0.0), axis=1, keepdims=True
+            )
+            back_scales.append(jnp.log(first) + back_scales[b])
+
+    scale_row = zero
+    for b in range(BLOCKS):
+        scale_row = jnp.where(row_col // 8 == b, scales[b], scale_row)
+    forward_row = jnp.log(row_of(sums)) + scale_row
     return jnp.where(row_lane < 64, forward_row, back_sums)
 
 
@@ -514,8 +545,8 @@
     dosage, like = pl.pallas_call(
         functools.partial(kernel, n_y, n_z, k),
         out_shape=(
-            jax.ShapeDtypeStruct((2, BLOCK), F32),
-            jax.ShapeDtypeStruct((1, 2), F32),
+            pltpu.VMEM((2, BLOCK), F32),
+            pltpu.VMEM((1, 2), F32),
         ),
         in_specs=[
             pl.BlockSpec(memory_space=pl.ANY),

time: 44.8 us -> 43.4 us (0.969)
  local copies, waits for them, and re-layouts: 1.8 us -> 1.08 us
  Pallas kernels: 42.2 us -> 41.5 us
    unnamed x6 -> x2, local copies, waits for them, and re-layouts: 1.8 us -> 1.08 us
    pallas_call x1, Pallas kernels: 42.2 us -> 41.5 us  [on_device(): pl.pallas_call(functools.partial(kernel, n_y, n_z, k), out_shape=(pltpu.V...]
where the time goes in v3:
time: 43.4 us; the launch traced here: 43.3 us
  Pallas kernels  41.5 us (96%)
  local copies, waits for them, and re-layouts  1.08 us (2%)
  between operations  0.64 us (1%)
    pallas_call x1, Pallas kernels, on_device(): pl.pallas_call(functools.partial(kernel, n_y, n_z, k), out_shape=(pltpu.V...  41.5 us
    unnamed x2, local copies, waits for them, and re-layouts  1.08 us

profile of v3, /device:TPU:1, one launch (start us, length us, event | category | flops | bytes accessed | tf_op | source)
XLA Modules:
  0.0 43.3 jit_solution(10769932718228659902)
XLA Ops:
  0.6 41.5 %shard_map.50 = (f32[2,8]{1,0:T(2,128)S(1)}, f32[1,2]{1,0:T(1,128)S(1)}) custom-call(s32[8,4096]{1,0:T(8,128)} %panel_ref.1, f32[1,8]{1,0:T(1,128)} %bitcast.3, s32[2,8]{1,0:T(2,128)} %geno_ref.1), custom_call_target="tpu_custom_call" | custom-call | tf_op jit(solution)/shard_map/pallas_call | solution.py:545
  42.2 0.6 %copy.7 = f32[2,8]{1,0:T(2,128)} copy(f32[2,8]{1,0:T(2,128)S(1)} %get-tuple-element.6) | data formatting | bytes 128
  42.7 0.5 %copy.8 = f32[2]{0:T(128)} copy(f32[2]{0:T(128)S(1)} %bitcast.2) | data formatting | bytes 16

commit v4 on v3

--- a/solution.py
+++ b/solution.py
@@ -66,6 +66,13 @@
     return jnp.where(row < 64, upper, lower).astype(BF16)
 
 
+def product(a, b):
+    a_top, b_top = a.astype(BF16), b.astype(BF16)
+    a_rest = (a - a_top.astype(F32)).astype(BF16)
+    b_rest = (b - b_top.astype(F32)).astype(BF16)
+    return dot_nt(a_top, b_top) + (dot_nt(a_rest, b_top) + dot_nt(a_top, b_rest))
+
+
 def couplings(signs, genotype):
     width = signs.shape[1]
     sign = jnp.where(genotype == 2.0, 0.0, 2.0 * genotype - 1.0)
@@ -73,14 +80,14 @@
     from_s, to_t = steps[:64], steps[64:]
     u = jnp.exp(STEP * from_s)
     v = jnp.exp(STEP * to_t)
-    full = jnp.log(dot_nt(u, jnp.concatenate([v, v], axis=0), HIGHEST))
+    full = jnp.log(product(u, jnp.concatenate([v, v], axis=0)))
     left, right = from_s[16:17], to_t[47:48]
     middle = left + right
     top = jnp.max(middle, axis=1, keepdims=True)
     begin = jnp.exp(STEP * (from_s[:16] - left + (middle - top)))
     end = jnp.exp(STEP * (to_t[48:] - right))
     blank = jnp.zeros((48, width), F32)
-    corner = jnp.log(dot_nt(begin, jnp.concatenate([blank, end, blank, end], axis=0), HIGHEST))
+    corner = jnp.log(product(begin, jnp.concatenate([blank, end, blank, end], axis=0)))
     corner = corner + STEP * top
     return pack(full, corner)
 
@@ -104,11 +111,15 @@
         )
     first = jnp.where(lane < 64, pairs[0], pairs[1])
     second = jnp.where(lane < 64, pairs[2], pairs[3])
-    return jnp.concatenate([first, second, diagonal], axis=0)
+    halves = jnp.where(lane < 64, diagonal, pltpu.roll(diagonal, 4, 0))
+    return jnp.concatenate([first, second, halves], axis=0)
 
 
 def unpack(packed):
-    first, second, diagonal = packed[0:8], packed[8:16], packed[16:24]
+    first, second, halves = packed[0:8], packed[8:16], packed[16:24]
+    diagonal = jnp.where(
+        iota((8, 128), 0) < 4, low_half(halves), pltpu.roll(high_half(halves), 4, 0)
+    )
     pairs = [low_half(first), high_half(first), low_half(second), high_half(second)]
     rows = [None] * BLOCKS
     for a in range(4):
@@ -259,38 +270,36 @@
     return jnp.where(row_lane < 64, forward_row, back_sums)
 
 
-def by_target(first, second):
-    return jnp.where(iota((8, 128), 0) < 4, first, second)
-
-
-def emission_terms(geno_rows):
-    g = by_target(geno_rows[0], geno_rows[1])
+def emission_terms(geno_row):
+    g = geno_row
     base = jnp.where(g == 2.0, 1.0, jnp.where(g == 1.0, DOWN, UP))
     slope = jnp.where(g == 2.0, 0.0, jnp.where(g == 1.0, UP - DOWN, DOWN - UP))
     return base, slope
 
 
-def state_terms(solved, rate_row, k):
-    lane = iota((8, 128), 1)
-    logs = by_target(solved[0], solved[1])
+def state_terms(logs, rate_row, k):
+    lane = iota((1, 128), 1)
     before = jnp.where(lane == 0, 0.0, pltpu.roll(logs, 1, 1))
     after = jnp.where(lane == 127, 0.0, pltpu.roll(logs, 127, 1))
     over_forward = jnp.exp(before - logs)
     over_backward = pltpu.roll(jnp.exp(after - logs), 64, 1)
     keep = 1.0 - rate_row
     jump = rate_row * (1.0 / k)
-    return (
-        keep * over_forward,
-        jump * over_forward,
-        keep * over_backward,
-        jnp.broadcast_to(jump, (8, 128)),
-    )
+    rows = (keep * over_forward, jump * over_forward, keep * over_backward, jump)
+    return [jnp.broadcast_to(row, (8, 128)) for row in rows]
+
+
+def interleave(first, second):
+    lane = iota((1, 128), 1)
+    first = first + pltpu.roll(first, 127, 1)
+    second = second + pltpu.roll(second, 127, 1)
+    return jnp.where(lane % 2 == 0, first, pltpu.roll(second, 1, 1))
 
 
 def dosage_of(total):
     lane = iota((8, 128), 1)
     sub = iota((8, 128), 0)
-    picked = jnp.where((lane // 4) % 2 == sub, total, 0.0)
+    picked = jnp.where(lane % 2 == sub, total, 0.0)
     src = iota((128, 128), 0)
     dst = iota((128, 128), 1)
     upper = ((src // 8 == dst) & (src < 64)).astype(F32)
@@ -300,21 +309,27 @@
     return numerator[0:2, 0:8] / denominator[0:2, 0:8]
 
 
+def far_first(n):
+    return sorted(range(1, n), key=lambda d: -min(d, n - d))
+
+
 def kernel(
     n_y, n_z, k,
     panel_ref, rate_ref, geno_ref,
     dosage_ref, like_ref,
-    panel_all, meta_all, tiles, emis, fwd, bwd,
-    log_send, log_group, log_mid, log_y, log_last, log_z,
+    panel_own, panel_all, meta_all, tiles, emis, fwd, bwd,
+    log_send, log_plane, log_mid, log_z, log_last,
     solve_send, solve_recv, sum_send, sum_group, sum_mid, sum_batch,
-    own_sem, tile_sem,
-    panel_s, panel_r, meta_s, meta_r, group_s, group_r, y_s, y_r, z_s, z_r,
-    core_s, core_r, group2_s, group2_r, batch_s, batch_r,
+    load_sem, own_sem, tile_sem, known,
+    panel_s, panel_r, meta_s, meta_r, plane_s, plane_r, z_s, z_r,
+    core_s, core_r, group_s, group_r, batch_s, batch_r,
 ):
     n_group = BLOCKS
+    n_x = n_group // 2
     group = lax.axis_index("group")
     batch = lax.axis_index("batch")
     core = group % 2
+    x = group // 2
     y = batch % n_y
     z = batch // n_y
     width = panel_all.shape[2]
@@ -332,23 +347,8 @@
     def z_peer(d):
         return (group, ((z + d) % n_z) * n_y + y)
 
-    def far_first(n):
-        return sorted(range(1, n), key=lambda d: -min(d, n - d))
-
-    barrier = pltpu.get_barrier_semaphore()
-    peers = [group_peer(d) for d in far_first(n_group)]
-    peers += [z_peer(d) for d in far_first(n_z)]
-    peers += [y_peer(d) for d in far_first(n_y)]
-    for peer in peers:
-        pl.semaphore_signal(barrier, inc=1, device_id=peer, device_id_type=MESH)
-    own_panel = pltpu.make_async_copy(
-        panel_ref.at[:, pl.ds(pl.multiple_of(group * width, width), width)],
-        panel_all.at[group],
-        own_sem,
-    )
-    own_panel.start()
-    meta_all[group] = meta_tile(rate_ref[...], geno_ref[...])
-    pl.semaphore_wait(barrier, len(peers))
+    def plane_peer(dx, dy):
+        return (((x + dx) % n_x) * 2 + core, z * n_y + (y + dy) % n_y)
 
     def remote(src, dst, send, recv, peer):
         return pltpu.make_async_remote_copy(
@@ -356,15 +356,38 @@
             device_id=peer, device_id_type=MESH,
         )
 
+    def finish(copies):
+        for copy in copies:
+            copy.wait()
+
+    load = pltpu.make_async_copy(panel_ref, panel_own, load_sem)
+    load.start()
+    own = pltpu.make_async_copy(
+        panel_ref.at[:, pl.ds(pl.multiple_of(x * width, width), width)],
+        panel_all.at[group],
+        own_sem,
+    )
+    own.start()
+    barrier = pltpu.get_barrier_semaphore()
+    near_y = [y_peer(d) for d in sorted({1, n_y - 1}) if 0 < d < n_y]
+    near_z = [z_peer(d) for d in sorted({1, n_z - 1}) if 0 < d < n_z]
+    peers = [group_peer(d) for d in far_first(n_group)] + near_y + near_z
+    for peer in peers:
+        pl.semaphore_signal(barrier, inc=1, device_id=peer, device_id_type=MESH)
+    meta_all[group] = meta_tile(rate_ref[...], geno_ref[...])
+    load.wait()
+    pl.semaphore_wait(barrier, len(peers))
+
     copies = []
     for d in far_first(n_group):
-        start = pl.multiple_of(in_group(d) * width, width)
+        start = pl.multiple_of(in_group(d) // 2 * width, width)
         copies.append(
             remote(
-                panel_ref.at[:, pl.ds(start, width)], panel_all.at[group],
+                panel_own.at[:, pl.ds(start, width)], panel_all.at[group],
                 panel_s.at[d - 1], panel_r.at[d - 1], group_peer(d),
             )
         )
+    for d in far_first(n_group):
         copies.append(
             remote(
                 meta_all.at[group], meta_all.at[group],
@@ -373,94 +396,73 @@
         )
     for copy in copies:
         copy.start()
-    own_panel.wait()
-    for copy in copies:
-        copy.wait()
+    for turn, near in enumerate([near_y + near_z, near_y + near_z, near_z]):
+        for peer in near:
+            pl.semaphore_signal(known.at[turn], inc=1, device_id=peer, device_id_type=MESH)
+        if near:
+            pl.semaphore_wait(known.at[turn], len(near))
+    own.wait()
+    finish(copies)
 
     relayout = []
-    for c in range(4):
-        for h in range(2):
-            copy = pltpu.make_async_copy(
-                panel_all.at[:, :, pl.ds(128 * c, 128)],
-                tiles.at[:, :, 4 * h + c],
-                tile_sem.at[4 * h + c],
-            )
-            copy.start()
-            relayout.append(copy)
+    for c in range(8):
+        copy = pltpu.make_async_copy(
+            panel_all.at[:, :, pl.ds(128 * c, 128)], tiles.at[:, :, c], tile_sem.at[c]
+        )
+        copy.start()
+        relayout.append(copy)
 
     meta = meta_all[...].reshape(MARKERS, 128)
     signs = 2.0 * panel_all[...].reshape(MARKERS, width).astype(F32) - 1.0
-    for h in range(2):
-        log_send[h] = couplings(signs, meta[:, 1 + h : 2 + h])
-
-    def start_all(n, order, src, slots, send, recv, peer):
-        out = [
-            remote(src(d), slots.at[d - 1], send.at[d - 1], recv.at[d - 1], peer(d)) for d in order
-        ]
-        for copy in out:
-            copy.start()
-        return out
-
-    def finish(copies):
-        for copy in copies:
-            copy.wait()
-
-    flying = start_all(
-        n_group, far_first(n_group), lambda d: log_send.at[in_group(d) % 2],
-        log_group, group_s, group_r, group_peer,
-    )
+    genotype = jnp.where(core == 0, meta[:, 1:2], meta[:, 2:3])
+    log_send[...] = couplings(signs, genotype)
+    sent = pl.ds(0, 20)
+
+    plane = [(dx, dy) for dx in range(n_x) for dy in range(n_y) if dx or dy]
+    plane.sort(key=lambda p: -(min(p[0], n_x - p[0]) + min(p[1], n_y - p[1])))
+    flying = [
+        remote(
+            log_send.at[sent], log_plane.at[i], plane_s.at[i], plane_r.at[i], plane_peer(dx, dy)
+        )
+        for i, (dx, dy) in enumerate(plane)
+    ]
+    for copy in flying:
+        copy.start()
     rates = [meta[8 * a : 8 * a + 8, 0:1] for a in range(BLOCKS)]
     terms = rate_terms(rates, log_k)
     rate_row = row_of(rates)
-    geno_rows = [
-        row_of([meta[8 * a : 8 * a + 8, 1 + h : 2 + h] for a in range(BLOCKS)]) for h in range(2)
-    ]
+    geno_row = row_of([genotype[8 * a : 8 * a + 8] for a in range(BLOCKS)])
+    base, slope = emission_terms(geno_row)
+    log_mid[...] = jnp.zeros((24, 128), F32)
+    log_last[...] = jnp.zeros((24, 128), F32)
     finish(flying)
-    total = log_total([log_send[core]] + [log_group[d] for d in range(n_group - 1)])
-    if n_y > 1:
-        log_mid[...] = total
-        flying = start_all(
-            n_y, far_first(n_y), lambda d: log_mid, log_y, y_s, y_r, y_peer
-        )
-        finish(flying)
-        total = log_total([total] + [log_y[d] for d in range(n_y - 1)])
-    base, slope = emission_terms(geno_rows)
-
-    def emissions():
-        finish(relayout)
-        for t in range(MARKERS):
-            allele = tiles[t // 8, t % 8].astype(F32)
-            emis[t] = base[:, t : t + 1] + slope[:, t : t + 1] * allele
-
-    if n_z > 1:
-        log_last[...] = total
-        flying = start_all(
-            n_z, far_first(n_z), lambda d: log_last, log_z, z_s, z_r, z_peer
-        )
-        emissions()
-        finish(flying)
-        total = log_total([total] + [log_z[d] for d in range(n_z - 1)])
-    else:
-        emissions()
-
-    mine = solve(total, terms, log_k)
-    solve_send[...] = mine
+    total = log_total([log_send[0:20]] + [log_plane[i] for i in range(len(plane))])
+    log_mid[0:20] = total
+
+    flying = [
+        remote(log_mid.at[sent], log_z.at[d - 1], z_s.at[d - 1], z_r.at[d - 1], z_peer(d))
+        for d in far_first(n_z)
+    ]
+    for copy in flying:
+        copy.start()
+    finish(relayout)
+    for t in range(MARKERS):
+        allele = tiles[t // 8, t % 8].astype(F32)
+        emis[t] = base[:, t : t + 1] + slope[:, t : t + 1] * allele
+    finish(flying)
+    log_last[0:20] = log_total([total] + [log_z[d] for d in range(n_z - 1)])
+
+    solved = solve(log_last[...], terms, log_k)
+
+    lane_row = iota((1, 128), 1)
+    seen = jnp.sum(
+        jnp.where((lane_row < 64) & (geno_row != 2.0), LOG_CENTRE, 0.0), axis=1, keepdims=True
+    )
+    like = jnp.broadcast_to((solved[:, 63:64] + seen) * (1.0 / MARKERS), (1, 128))
+    solve_send[...] = like
     partner = (group + 1 - 2 * core, batch)
     swap = remote(solve_send, solve_recv, core_s, core_r, partner)
     swap.start()
-    swap.wait()
-    theirs = solve_recv[...]
-    solved = [jnp.where(core == 0, mine, theirs), jnp.where(core == 0, theirs, mine)]
-
-    lane_row = iota((1, 128), 1)
-    likes = []
-    for h in range(2):
-        seen = jnp.sum(
-            jnp.where((lane_row < 64) & (geno_rows[h] != 2.0), LOG_CENTRE, 0.0),
-            axis=1, keepdims=True,
-        )
-        likes.append((solved[h][:, 63:64] + seen) * (1.0 / MARKERS))
-    like_ref[...] = jnp.where(lane_row == 0, likes[0], likes[1])[:, 0:2]
 
     keep_f, jump_f, keep_b, jump_b = state_terms(solved, rate_row, float(k))
     ahead = jnp.full((8, 128), 1.0 / k, F32)
@@ -482,14 +484,22 @@
         sums = dot_nt(ones, coarse) + dot_nt(ones, fine)
         sum_send[a] = sums[0:1]
 
-    flying = start_all(
-        n_group, far_first(n_group), lambda d: sum_send.at[in_group(d)],
-        sum_group, group2_s, group2_r, group_peer,
-    )
+    flying = [
+        remote(
+            sum_send.at[in_group(d)], sum_group.at[d - 1],
+            group_s.at[d - 1], group_r.at[d - 1], group_peer(d),
+        )
+        for d in far_first(n_group)
+    ]
+    for copy in flying:
+        copy.start()
     finish(flying)
-    total = functools.reduce(
-        jnp.add, [sum_send[group]] + [sum_group[d] for d in range(n_group - 1)]
-    )
+    mine = functools.reduce(jnp.add, [sum_send[group]] + [sum_group[d - 1] for d in (2, 4, 6)])
+    theirs = functools.reduce(jnp.add, [sum_group[d - 1] for d in (1, 3, 5, 7)])
+    total = interleave(
+        jnp.where(core == 0, mine, theirs), jnp.where(core == 0, theirs, mine)
+    )
+
     n_batch = n_y * n_z
     sum_mid[...] = total
     flying = [
@@ -502,6 +512,11 @@
     for copy in flying:
         copy.start()
     sum_batch[n_batch - 1 : n_batch] = total
+    swap.wait()
+    other = solve_recv[...]
+    like_ref[...] = jnp.where(
+        lane_row == 0, jnp.where(core == 0, like, other), jnp.where(core == 0, other, like)
+    )[:, 0:2]
     finish(flying)
     total = jnp.sum(sum_batch[...], axis=0, keepdims=True)
     dosage_ref[...] = dosage_of(total)
@@ -511,24 +526,25 @@
     n_batch = lax.axis_size("batch")
     n_group = lax.axis_size("group")
     n_z = n_batch // n_y
-    width = panel.shape[1] // n_group
-    k = panel.shape[1] * n_batch
+    held = panel.shape[1]
+    width = held // (n_group // 2)
+    k = held * n_batch
     dma = pltpu.SemaphoreType.DMA
     vmem = pltpu.VMEM
-    g1, y1, z1 = n_group - 1, max(n_y - 1, 1), max(n_z - 1, 1)
+    g1, z1, p1 = n_group - 1, max(n_z - 1, 1), n_group // 2 * n_y - 1
     scratch = [
+        vmem((BLOCK, held), jnp.int32),
         vmem((BLOCKS, BLOCK, width), jnp.int32),
         vmem((BLOCKS, BLOCK, 128), F32),
         vmem((BLOCKS, BLOCK, 8, 128), jnp.int32),
         vmem((MARKERS, 8, 128), F32),
         vmem((MARKERS, 8, 128), F32),
         vmem((MARKERS, 8, 128), F32),
-        vmem((2, 24, 128), F32),
-        vmem((g1, 24, 128), F32),
         vmem((24, 128), F32),
-        vmem((y1, 24, 128), F32),
+        vmem((p1, 20, 128), F32),
         vmem((24, 128), F32),
-        vmem((z1, 24, 128), F32),
+        vmem((z1, 20, 128), F32),
+        vmem((24, 128), F32),
         vmem((1, 128), F32),
         vmem((1, 128), F32),
         vmem((BLOCKS, 1, 128), F32),
@@ -536,9 +552,11 @@
         vmem((1, 128), F32),
         vmem((n_batch, 128), F32),
         dma,
+        dma,
         dma((8,)),
-        dma((g1,)), dma((g1,)), dma((g1,)), dma((g1,)), dma((g1,)), dma((g1,)),
-        dma((y1,)), dma((y1,)), dma((z1,)), dma((z1,)),
+        pltpu.SemaphoreType.REGULAR((3,)),
+        dma((g1,)), dma((g1,)), dma((g1,)), dma((g1,)), dma((p1,)), dma((p1,)),
+        dma((z1,)), dma((z1,)),
         dma, dma,
         dma((g1,)), dma((g1,)), dma((n_batch - 1,)), dma((n_batch - 1,)),
     ]

time: 43.4 us -> 40.7 us (0.938)
  Pallas kernels: 41.5 us -> 38.8 us
    pallas_call x1, Pallas kernels: 41.5 us -> 38.8 us  [on_device(): pl.pallas_call(functools.partial(kernel, n_y, n_z, k), out_shape=(pltpu.V...]
where the time goes in v4:
time: 40.7 us; the launch traced here: 40.6 us
  Pallas kernels  38.8 us (95%)
  local copies, waits for them, and re-layouts  1.08 us (3%)
  between operations  0.64 us (2%)
    pallas_call x1, Pallas kernels, on_device(): pl.pallas_call(functools.partial(kernel, n_y, n_z, k), out_shape=(pltpu.V...  38.8 us
    unnamed x2, local copies, waits for them, and re-layouts  1.08 us

profile of v4, /device:TPU:1, one launch (start us, length us, event | category | flops | bytes accessed | tf_op | source)
XLA Modules:
  0.0 40.6 jit_solution(2010685261904244744)
XLA Ops:
  0.6 38.8 %shard_map.50 = (f32[2,8]{1,0:T(2,128)S(1)}, f32[1,2]{1,0:T(1,128)S(1)}) custom-call(s32[8,4096]{1,0:T(8,128)} %panel_ref.1, f32[1,8]{1,0:T(1,128)} %bitcast.3, s32[2,8]{1,0:T(2,128)} %geno_ref.1), custom_call_target="tpu_custom_call" | custom-call | tf_op jit(solution)/shard_map/pallas_call | solution.py:563
  39.5 0.6 %copy.7 = f32[2,8]{1,0:T(2,128)} copy(f32[2,8]{1,0:T(2,128)S(1)} %get-tuple-element.6) | data formatting | bytes 128
  40.0 0.5 %copy.8 = f32[2]{0:T(128)} copy(f32[2]{0:T(128)S(1)} %bitcast.2) | data formatting | bytes 16

commit v5 on v4

--- a/solution.py
+++ b/solution.py
@@ -289,24 +289,26 @@
     return [jnp.broadcast_to(row, (8, 128)) for row in rows]
 
 
-def interleave(first, second):
-    lane = iota((1, 128), 1)
-    first = first + pltpu.roll(first, 127, 1)
-    second = second + pltpu.roll(second, 127, 1)
-    return jnp.where(lane % 2 == 0, first, pltpu.roll(second, 1, 1))
-
-
-def dosage_of(total):
-    lane = iota((8, 128), 1)
+def gather_sublanes(tiles):
     sub = iota((8, 128), 0)
-    picked = jnp.where(lane % 2 == sub, total, 0.0)
-    src = iota((128, 128), 0)
-    dst = iota((128, 128), 1)
-    upper = ((src // 8 == dst) & (src < 64)).astype(F32)
-    lower = (src // 8 == dst + 8).astype(F32)
-    numerator = jnp.dot(picked, upper, precision=HIGHEST, preferred_element_type=F32)
-    denominator = jnp.dot(picked, lower, precision=HIGHEST, preferred_element_type=F32)
-    return numerator[0:2, 0:8] / denominator[0:2, 0:8]
+    step = 4
+    while len(tiles) > 1:
+        half = len(tiles) // 2
+        low = sub & step == 0
+        merged = []
+        for i in range(half):
+            first, second = tiles[i], tiles[i + half]
+            kept = jnp.where(low, first, second)
+            moved = jnp.where(low, second, first)
+            merged.append(kept + pltpu.roll(moved, step, 0) if step == 4 else kept + swap_by(moved, step))
+        tiles = merged
+        step //= 2
+    return tiles[0]
+
+
+def swap_by(x, step):
+    low = iota((8, 128), 0) & step == 0
+    return jnp.where(low, pltpu.roll(x, 8 - step, 0), pltpu.roll(x, step, 0))
 
 
 def far_first(n):
@@ -317,12 +319,12 @@
     n_y, n_z, k,
     panel_ref, rate_ref, geno_ref,
     dosage_ref, like_ref,
-    panel_own, panel_all, meta_all, tiles, emis, fwd, bwd,
+    rate_own, geno_own, panel_own, panel_all, meta_all, tiles, emis, fwd, bwd,
     log_send, log_plane, log_mid, log_z, log_last,
-    solve_send, solve_recv, sum_send, sum_group, sum_mid, sum_batch,
+    solve_send, solve_recv, sum_send, sum_all, dose_send, dose_recv,
     load_sem, own_sem, tile_sem, known,
     panel_s, panel_r, meta_s, meta_r, plane_s, plane_r, z_s, z_r,
-    core_s, core_r, group_s, group_r, batch_s, batch_r,
+    core_s, core_r, all_s, all_r, dose_s, dose_r,
 ):
     n_group = BLOCKS
     n_x = n_group // 2
@@ -360,13 +362,18 @@
         for copy in copies:
             copy.wait()
 
-    load = pltpu.make_async_copy(panel_ref, panel_own, load_sem)
-    load.start()
+    loads = [
+        pltpu.make_async_copy(rate_ref, rate_own, load_sem.at[0]),
+        pltpu.make_async_copy(geno_ref, geno_own, load_sem.at[1]),
+        pltpu.make_async_copy(panel_ref, panel_own, load_sem.at[2]),
+    ]
     own = pltpu.make_async_copy(
         panel_ref.at[:, pl.ds(pl.multiple_of(x * width, width), width)],
         panel_all.at[group],
         own_sem,
     )
+    for load in loads:
+        load.start()
     own.start()
     barrier = pltpu.get_barrier_semaphore()
     near_y = [y_peer(d) for d in sorted({1, n_y - 1}) if 0 < d < n_y]
@@ -374,8 +381,8 @@
     peers = [group_peer(d) for d in far_first(n_group)] + near_y + near_z
     for peer in peers:
         pl.semaphore_signal(barrier, inc=1, device_id=peer, device_id_type=MESH)
-    meta_all[group] = meta_tile(rate_ref[...], geno_ref[...])
-    load.wait()
+    finish(loads)
+    meta_all[group] = meta_tile(rate_own[...], geno_own[...])
     pl.semaphore_wait(barrier, len(peers))
 
     copies = []
@@ -474,52 +481,53 @@
         bwd[t] = behind
         behind = keep_b[:, t : t + 1] * (emis[t] * behind) + jump_b[:, t : t + 1]
 
+    over_k = []
+    for which in range(2):
+        for a in range(BLOCKS):
+            both = fwd[8 * a : 8 * a + 8] * bwd[8 * a : 8 * a + 8]
+            if which == 0:
+                both = both * tiles[a].astype(F32)
+            over_k.append(gather_sublanes([both[i] for i in range(8)]))
+    stacked = jnp.concatenate(over_k, axis=0)
     ones = jnp.ones((8, 128), BF16)
-    for a in range(BLOCKS):
-        both = fwd[8 * a : 8 * a + 8] * bwd[8 * a : 8 * a + 8]
-        carrying = both * tiles[a].astype(F32)
-        stacked = jnp.concatenate([carrying.reshape(64, 128), both.reshape(64, 128)], axis=0)
-        coarse = stacked.astype(BF16)
-        fine = (stacked - coarse.astype(F32)).astype(BF16)
-        sums = dot_nt(ones, coarse) + dot_nt(ones, fine)
-        sum_send[a] = sums[0:1]
-
-    flying = [
-        remote(
-            sum_send.at[in_group(d)], sum_group.at[d - 1],
-            group_s.at[d - 1], group_r.at[d - 1], group_peer(d),
-        )
-        for d in far_first(n_group)
+    coarse = stacked.astype(BF16)
+    fine = (stacked - coarse.astype(F32)).astype(BF16)
+    total = (dot_nt(ones, coarse) + dot_nt(ones, fine))[0:1]
+
+    everyone = [
+        (dx, dy, dz) for dx in range(n_x) for dy in range(n_y) for dz in range(n_z)
+        if dx or dy or dz
     ]
-    for copy in flying:
-        copy.start()
-    finish(flying)
-    mine = functools.reduce(jnp.add, [sum_send[group]] + [sum_group[d - 1] for d in (2, 4, 6)])
-    theirs = functools.reduce(jnp.add, [sum_group[d - 1] for d in (1, 3, 5, 7)])
-    total = interleave(
-        jnp.where(core == 0, mine, theirs), jnp.where(core == 0, theirs, mine)
+    everyone.sort(
+        key=lambda p: -(min(p[0], n_x - p[0]) + min(p[1], n_y - p[1]) + min(p[2], n_z - p[2]))
     )
-
-    n_batch = n_y * n_z
-    sum_mid[...] = total
-    flying = [
-        remote(
-            sum_mid, sum_batch.at[pl.ds(d - 1, 1)], batch_s.at[d - 1], batch_r.at[d - 1],
-            (group, (batch + d) % n_batch),
-        )
-        for d in range(1, n_batch)
-    ]
-    for copy in flying:
-        copy.start()
-    sum_batch[n_batch - 1 : n_batch] = total
+    others = len(everyone)
+    sum_send[...] = total
+    for i, (dx, dy, dz) in enumerate(everyone):
+        peer = (
+            ((x + dx) % n_x) * 2 + core,
+            ((z + dz) % n_z) * n_y + (y + dy) % n_y,
+        )
+        remote(sum_send, sum_all.at[pl.ds(i, 1)], all_s, all_r, peer).start()
+    sum_all[others : others + 1] = total
     swap.wait()
     other = solve_recv[...]
     like_ref[...] = jnp.where(
         lane_row == 0, jnp.where(core == 0, like, other), jnp.where(core == 0, other, like)
     )[:, 0:2]
-    finish(flying)
-    total = jnp.sum(sum_batch[...], axis=0, keepdims=True)
-    dosage_ref[...] = dosage_of(total)
+    rest = pl.ds(0, others)
+    remote(sum_all.at[rest], sum_all.at[rest], all_s, all_r, partner).wait()
+    total = jnp.sum(sum_all[...], axis=0, keepdims=True)
+    share = total / pltpu.roll(total, 64, 1)
+    dose_send[...] = share
+    trade = remote(dose_send, dose_recv, dose_s, dose_r, partner)
+    trade.start()
+    shift = (128 - 8 * group) % 128
+    mine = pltpu.roll(share, shift, 1)
+    trade.wait()
+    theirs = pltpu.roll(dose_recv[...], shift, 1)
+    dosage_ref[0:1] = jnp.where(core == 0, mine, theirs)[:, 0:8]
+    dosage_ref[1:2] = jnp.where(core == 0, theirs, mine)[:, 0:8]
 
 
 def on_device(n_y, panel, rates, genotypes):
@@ -533,6 +541,8 @@
     vmem = pltpu.VMEM
     g1, z1, p1 = n_group - 1, max(n_z - 1, 1), n_group // 2 * n_y - 1
     scratch = [
+        vmem((1, BLOCK), F32),
+        vmem((2, BLOCK), jnp.int32),
         vmem((BLOCK, held), jnp.int32),
         vmem((BLOCKS, BLOCK, width), jnp.int32),
         vmem((BLOCKS, BLOCK, 128), F32),
@@ -547,18 +557,18 @@
         vmem((24, 128), F32),
         vmem((1, 128), F32),
         vmem((1, 128), F32),
-        vmem((BLOCKS, 1, 128), F32),
-        vmem((g1, 1, 128), F32),
         vmem((1, 128), F32),
-        vmem((n_batch, 128), F32),
-        dma,
+        vmem((n_group // 2 * n_batch, 128), F32),
+        vmem((1, 128), F32),
+        vmem((1, 128), F32),
+        dma((3,)),
         dma,
         dma((8,)),
         pltpu.SemaphoreType.REGULAR((3,)),
         dma((g1,)), dma((g1,)), dma((g1,)), dma((g1,)), dma((p1,)), dma((p1,)),
         dma((z1,)), dma((z1,)),
         dma, dma,
-        dma((g1,)), dma((g1,)), dma((n_batch - 1,)), dma((n_batch - 1,)),
+        dma, dma, dma, dma,
     ]
     dosage, like = pl.pallas_call(
         functools.partial(kernel, n_y, n_z, k),
@@ -568,8 +578,8 @@
         ),
         in_specs=[
             pl.BlockSpec(memory_space=pl.ANY),
-            pl.BlockSpec(memory_space=pltpu.VMEM),
-            pl.BlockSpec(memory_space=pltpu.VMEM),
+            pl.BlockSpec(memory_space=pl.ANY),
+            pl.BlockSpec(memory_space=pl.ANY),
         ],
         out_specs=(
             pl.BlockSpec(memory_space=pltpu.VMEM),

time: 40.7 us -> 39.1 us (0.961)
  Pallas kernels: 38.8 us -> 37.3 us
    pallas_call x1, Pallas kernels: 38.8 us -> 37.3 us  [on_device(): pl.pallas_call(functools.partial(kernel, n_y, n_z, k), out_shape=(pltpu.V...]
where the time goes in v5:
time: 39.1 us; the launch traced here: 39 us
  Pallas kernels  37.3 us (95%)
  local copies, waits for them, and re-layouts  1.08 us (3%)
  between operations  0.64 us (2%)
    pallas_call x1, Pallas kernels, on_device(): pl.pallas_call(functools.partial(kernel, n_y, n_z, k), out_shape=(pltpu.V...  37.3 us
    unnamed x2, local copies, waits for them, and re-layouts  1.08 us

profile of v5, /device:TPU:1, one launch (start us, length us, event | category | flops | bytes accessed | tf_op | source)
XLA Modules:
  0.0 39.0 jit_solution(13721301365927284620)
XLA Ops:
  0.6 37.3 %shard_map.50 = (f32[2,8]{1,0:T(2,128)S(1)}, f32[1,2]{1,0:T(1,128)S(1)}) custom-call(s32[8,4096]{1,0:T(8,128)} %panel_ref.1, f32[1,8]{1,0:T(1,128)} %bitcast.3, s32[2,8]{1,0:T(2,128)} %geno_ref.1), custom_call_target="tpu_custom_call" | custom-call | tf_op jit(solution)/shard_map/pallas_call | solution.py:573
  37.9 0.6 %copy.7 = f32[2,8]{1,0:T(2,128)} copy(f32[2,8]{1,0:T(2,128)S(1)} %get-tuple-element.6) | data formatting | bytes 128
  38.5 0.5 %copy.8 = f32[2]{0:T(128)} copy(f32[2]{0:T(128)S(1)} %bitcast.2) | data formatting | bytes 16

commit v6 on v5

--- a/solution.py
+++ b/solution.py
@@ -208,55 +208,58 @@
     for step in (1, 2, 4):
         offset = offset + pltpu.roll(offset, step, 1)
     factors = [jnp.exp(paths[a] - offset[a : a + 1]) for a in range(BLOCKS)]
-    jumps = [jnp.broadcast_to(jnp.exp(j), (8, 128)) for j in jump_col]
-    jumps_row = jnp.exp(jump_row)
-
+    injectors = [jnp.exp(j) * f for j, f in zip(jump_col, factors)]
     row_lane = iota((1, 128), 1)
     row_col = row_lane % 64
+    jumps_row = jnp.where(row_lane == 64, math.exp(-log_k), jnp.exp(jump_row))
+    shifted = [pltpu.roll(f, 1, 1) * jumps_row for f in factors]
+    shifted_offset = pltpu.roll(offset, 1, 1)
+    inverses = [jnp.where(block == b, forward_inverse, 0.0) for b in range(BLOCKS)]
+
     zero = jnp.zeros((1, 128), F32)
-
     sums = []
     scales = [zero, zero]
     last = jnp.ones((1, 128), F32)
     spent = jnp.zeros((8, 128), F32)
     scale_col = jnp.zeros((8, 128), F32)
-
-    back = zero
+    newest = None
+
     back_scales = [zero, zero]
     back_scale_row = zero
     back_sums = zero
-    behind_row = jnp.where(row_lane == 63, math.exp(-log_k), 0.0)
+    behind_row = jnp.where(row_lane == 64, 1.0, 0.0)
 
     for b in range(BLOCKS):
-        entering = last * jumps[b][0:1]
-        lead = entering * factors[b][0:1]
+        lead = last * injectors[b][0:1]
+        if b > 1:
+            weight = jnp.exp(offset + scale_col - scales[b])
+            weight = jnp.where((sub < b - 1) & (block == b), weight, 0.0)
+            lead = lead + jnp.sum(weight * spent, axis=0, keepdims=True)
         if b:
-            weight = jnp.where(sub < b, jnp.exp(offset + scale_col - scales[b]), 0.0)
-            lead = lead + jnp.sum(weight * spent, axis=0, keepdims=True)
-        here = jnp.sum(
-            jnp.where(block == b, lead * forward_inverse, 0.0), axis=1, keepdims=True
-        )
+            weight = jnp.exp(offset[b - 1 : b] + (scales[b - 1] - scales[b]))
+            weight = jnp.where(row_col // 8 == b, weight, 0.0)
+            lead = lead + weight * newest
+        here = jnp.sum(lead * inverses[b], axis=1, keepdims=True)
         here = jnp.broadcast_to(here, (8, 128))
         sums.append(here)
-        injected = jumps[b] * jnp.where(sub == 0, last, pltpu.roll(here, 1, 0))
         if b < BLOCKS - 1:
-            spent = jnp.where(
-                sub == b, jnp.sum(injected * factors[b], axis=0, keepdims=True), spent
-            )
+            before = jnp.where(sub == 0, last, pltpu.roll(here, 1, 0))
+            newest = jnp.sum(before * injectors[b], axis=0, keepdims=True)
+            spent = jnp.where(sub == b, newest, spent)
             scale_col = jnp.where(sub == b, scales[b], scale_col)
             last = here[7:8] * jnp.exp(scales[b] - scales[b + 1])
             scales.append(jnp.log(here[7:8]) + scales[b])
 
         c = BLOCKS - 1 - b
-        weight = jnp.exp(offset[c : c + 1] + back_scale_row - back_scales[b])
-        weight = jnp.where((row_lane >= 8 * c + 7) & (row_lane < 64), weight * behind_row, 0.0)
-        lead = jnp.sum(factors[c] * weight, axis=1, keepdims=True)
+        weight = jnp.exp(shifted_offset[c : c + 1] + (back_scale_row - back_scales[b]))
+        weight = jnp.where((row_lane >= 8 * c + 8) & (row_lane <= 64), weight, 0.0)
+        pulled = shifted[c] * weight
+        lead = jnp.sum(pulled * behind_row, axis=1, keepdims=True)
         back = jnp.sum(lead * backward_inverse, axis=0, keepdims=True)
+        inside = (row_lane >= 8 * c) & (row_lane < 8 * c + 8)
         back_sums = jnp.where(row_col // 8 == c, jnp.log(back) + back_scales[b], back_sums)
         if c:
-            fresh = pltpu.roll(back * jumps_row, 127, 1)
-            inside = (row_lane >= 8 * c - 1) & (row_lane <= 8 * c + 6)
-            behind_row = jnp.where(inside, fresh, behind_row)
+            behind_row = jnp.where(inside, back, behind_row)
             back_scale_row = jnp.where(inside, back_scales[b], back_scale_row)
             first = jnp.sum(
                 jnp.where(row_lane == 8 * c, back, 0.0), axis=1, keepdims=True
@@ -475,11 +478,12 @@
     ahead = jnp.full((8, 128), 1.0 / k, F32)
     behind = jnp.full((8, 128), 1.0 / k, F32)
     for i in range(MARKERS):
-        ahead = emis[i] * (keep_f[:, i : i + 1] * ahead + jump_f[:, i : i + 1])
+        kept, added = emis[i] * keep_f[:, i : i + 1], emis[i] * jump_f[:, i : i + 1]
+        ahead = kept * ahead + added
         fwd[i] = ahead
         t = MARKERS - 1 - i
         bwd[t] = behind
-        behind = keep_b[:, t : t + 1] * (emis[t] * behind) + jump_b[:, t : t + 1]
+        behind = (keep_b[:, t : t + 1] * emis[t]) * behind + jump_b[:, t : t + 1]
 
     over_k = []
     for which in range(2):

time: 39.1 us -> 38.6 us (0.987)
  Pallas kernels: 37.3 us -> 36.8 us
    pallas_call x1, Pallas kernels: 37.3 us -> 36.8 us  [on_device(): pl.pallas_call(functools.partial(kernel, n_y, n_z, k), out_shape=(pltpu.V...]
where the time goes in v6:
time: 38.6 us; the launch traced here: 38.5 us
  Pallas kernels  36.8 us (95%)
  local copies, waits for them, and re-layouts  1.08 us (3%)
  between operations  0.64 us (2%)
    pallas_call x1, Pallas kernels, on_device(): pl.pallas_call(functools.partial(kernel, n_y, n_z, k), out_shape=(pltpu.V...  36.8 us
    unnamed x2, local copies, waits for them, and re-layouts  1.08 us

profile of v6, /device:TPU:1, one launch (start us, length us, event | category | flops | bytes accessed | tf_op | source)
XLA Modules:
  0.0 38.5 jit_solution(17808744878879366176)
XLA Ops:
  0.6 36.8 %shard_map.50 = (f32[2,8]{1,0:T(2,128)S(1)}, f32[1,2]{1,0:T(1,128)S(1)}) custom-call(s32[8,4096]{1,0:T(8,128)} %panel_ref.1, f32[1,8]{1,0:T(1,128)} %bitcast.3, s32[2,8]{1,0:T(2,128)} %geno_ref.1), custom_call_target="tpu_custom_call" | custom-call | tf_op jit(solution)/shard_map/pallas_call | solution.py:577
  37.5 0.6 %copy.7 = f32[2,8]{1,0:T(2,128)} copy(f32[2,8]{1,0:T(2,128)S(1)} %get-tuple-element.6) | data formatting | bytes 128
  38.0 0.5 %copy.8 = f32[2]{0:T(128)} copy(f32[2]{0:T(128)S(1)} %bitcast.2) | data formatting | bytes 16

commit v7 on v6

--- a/solution.py
+++ b/solution.py
@@ -321,7 +321,7 @@
 def kernel(
     n_y, n_z, k,
     panel_ref, rate_ref, geno_ref,
-    dosage_ref, like_ref,
+    out_ref,
     rate_own, geno_own, panel_own, panel_all, meta_all, tiles, emis, fwd, bwd,
     log_send, log_plane, log_mid, log_z, log_last,
     solve_send, solve_recv, sum_send, sum_all, dose_send, dose_recv,
@@ -337,6 +337,7 @@
     x = group // 2
     y = batch % n_y
     z = batch // n_y
+    partner = (group + 1 - 2 * core, batch)
     width = panel_all.shape[2]
     log_k = math.log(k)
 
@@ -364,6 +365,12 @@
     def finish(copies):
         for copy in copies:
             copy.wait()
+
+    def hear(near, turn):
+        for peer in near:
+            pl.semaphore_signal(known.at[turn], inc=1, device_id=peer, device_id_type=MESH)
+        if near:
+            pl.semaphore_wait(known.at[turn], len(near))
 
     loads = [
         pltpu.make_async_copy(rate_ref, rate_own, load_sem.at[0]),
@@ -394,25 +401,25 @@
         copies.append(
             remote(
                 panel_own.at[:, pl.ds(start, width)], panel_all.at[group],
-                panel_s.at[d - 1], panel_r.at[d - 1], group_peer(d),
+                panel_s, panel_r, group_peer(d),
             )
         )
     for d in far_first(n_group):
         copies.append(
             remote(
                 meta_all.at[group], meta_all.at[group],
-                meta_s.at[d - 1], meta_r.at[d - 1], group_peer(d),
+                meta_s, meta_r, group_peer(d),
             )
         )
     for copy in copies:
         copy.start()
-    for turn, near in enumerate([near_y + near_z, near_y + near_z, near_z]):
-        for peer in near:
-            pl.semaphore_signal(known.at[turn], inc=1, device_id=peer, device_id_type=MESH)
-        if near:
-            pl.semaphore_wait(known.at[turn], len(near))
+    hear(near_y + near_z, 0)
+    hear(near_y + near_z, 1)
+    hear(near_z, 2)
     own.wait()
-    finish(copies)
+    most = pl.ds(0, n_group - 1)
+    remote(meta_all.at[most], meta_all.at[most], meta_s, meta_r, partner).wait()
+    remote(panel_all.at[most], panel_all.at[most], panel_s, panel_r, partner).wait()
 
     relayout = []
     for c in range(8):
@@ -432,7 +439,7 @@
     plane.sort(key=lambda p: -(min(p[0], n_x - p[0]) + min(p[1], n_y - p[1])))
     flying = [
         remote(
-            log_send.at[sent], log_plane.at[i], plane_s.at[i], plane_r.at[i], plane_peer(dx, dy)
+            log_send.at[sent], log_plane.at[i], plane_s, plane_r, plane_peer(dx, dy)
         )
         for i, (dx, dy) in enumerate(plane)
     ]
@@ -445,12 +452,12 @@
     base, slope = emission_terms(geno_row)
     log_mid[...] = jnp.zeros((24, 128), F32)
     log_last[...] = jnp.zeros((24, 128), F32)
-    finish(flying)
+    remote(log_plane, log_plane, plane_s, plane_r, partner).wait()
     total = log_total([log_send[0:20]] + [log_plane[i] for i in range(len(plane))])
     log_mid[0:20] = total
 
     flying = [
-        remote(log_mid.at[sent], log_z.at[d - 1], z_s.at[d - 1], z_r.at[d - 1], z_peer(d))
+        remote(log_mid.at[sent], log_z.at[d - 1], z_s, z_r, z_peer(d))
         for d in far_first(n_z)
     ]
     for copy in flying:
@@ -459,7 +466,8 @@
     for t in range(MARKERS):
         allele = tiles[t // 8, t % 8].astype(F32)
         emis[t] = base[:, t : t + 1] + slope[:, t : t + 1] * allele
-    finish(flying)
+    if n_z > 1:
+        remote(log_z, log_z, z_s, z_r, partner).wait()
     log_last[0:20] = log_total([total] + [log_z[d] for d in range(n_z - 1)])
 
     solved = solve(log_last[...], terms, log_k)
@@ -470,7 +478,6 @@
     )
     like = jnp.broadcast_to((solved[:, 63:64] + seen) * (1.0 / MARKERS), (1, 128))
     solve_send[...] = like
-    partner = (group + 1 - 2 * core, batch)
     swap = remote(solve_send, solve_recv, core_s, core_r, partner)
     swap.start()
 
@@ -516,7 +523,7 @@
     sum_all[others : others + 1] = total
     swap.wait()
     other = solve_recv[...]
-    like_ref[...] = jnp.where(
+    out_ref[2:3, 0:2] = jnp.where(
         lane_row == 0, jnp.where(core == 0, like, other), jnp.where(core == 0, other, like)
     )[:, 0:2]
     rest = pl.ds(0, others)
@@ -530,8 +537,13 @@
     mine = pltpu.roll(share, shift, 1)
     trade.wait()
     theirs = pltpu.roll(dose_recv[...], shift, 1)
-    dosage_ref[0:1] = jnp.where(core == 0, mine, theirs)[:, 0:8]
-    dosage_ref[1:2] = jnp.where(core == 0, theirs, mine)[:, 0:8]
+    out_ref[0:1, 0:8] = jnp.where(core == 0, mine, theirs)[:, 0:8]
+    out_ref[1:2, 0:8] = jnp.where(core == 0, theirs, mine)[:, 0:8]
+
+
+def hand_over(out_ref, dosage_ref, like_ref):
+    dosage_ref[...] = out_ref[0:2, 0:8]
+    like_ref[...] = out_ref[2:3, 0:2]
 
 
 def on_device(n_y, panel, rates, genotypes):
@@ -569,29 +581,30 @@
         dma,
         dma((8,)),
         pltpu.SemaphoreType.REGULAR((3,)),
-        dma((g1,)), dma((g1,)), dma((g1,)), dma((g1,)), dma((p1,)), dma((p1,)),
-        dma((z1,)), dma((z1,)),
+        dma, dma, dma, dma, dma, dma,
+        dma, dma,
         dma, dma,
         dma, dma, dma, dma,
     ]
-    dosage, like = pl.pallas_call(
+    out = pl.pallas_call(
         functools.partial(kernel, n_y, n_z, k),
-        out_shape=(
-            pltpu.VMEM((2, BLOCK), F32),
-            pltpu.VMEM((1, 2), F32),
-        ),
+        out_shape=pltpu.VMEM((8, 128), F32),
         in_specs=[
             pl.BlockSpec(memory_space=pl.ANY),
             pl.BlockSpec(memory_space=pl.ANY),
             pl.BlockSpec(memory_space=pl.ANY),
         ],
-        out_specs=(
-            pl.BlockSpec(memory_space=pltpu.VMEM),
-            pl.BlockSpec(memory_space=pltpu.VMEM),
-        ),
+        out_specs=pl.BlockSpec(memory_space=pltpu.VMEM),
         scratch_shapes=scratch,
         compiler_params=pltpu.CompilerParams(collective_id=0, has_side_effects=True),
     )(panel, rates.reshape(1, BLOCK), genotypes)
+    dosage, like = pl.pallas_call(
+        hand_over,
+        out_shape=(
+            jax.ShapeDtypeStruct((2, BLOCK), F32),
+            jax.ShapeDtypeStruct((1, 2), F32),
+        ),
+    )(pltpu.with_memory_space_constraint(out, pltpu.VMEM))
     return dosage, like.reshape(2)
 
 

time: 38.6 us -> 37.5 us (0.972)
  local copies, waits for them, and re-layouts: 1.08 us -> 0 us
    unnamed x2 -> x0, local copies, waits for them, and re-layouts: 1.08 us -> none
    pallas_call x1 -> x2, Pallas kernels: 36.8 us -> 36.8 us  [the longest x1 36.2 us: on_device(): pl.pallas_call(functools.partial(kernel, n_y, n_z, k), out_shape=pltpu.VM...]
where the time goes in v7:
time: 37.5 us; the launch traced here: 37.4 us
  Pallas kernels  36.8 us (98%)
  between operations  0.64 us (2%)
    pallas_call x1, Pallas kernels, on_device(): pl.pallas_call(functools.partial(kernel, n_y, n_z, k), out_shape=pltpu.VM...  36.2 us

profile of v7, /device:TPU:1, one launch (start us, length us, event | category | flops | bytes accessed | tf_op | source)
XLA Modules:
  0.0 37.4 jit_solution(6143478210399206970)
XLA Ops:
  0.6 36.2 %shard_map.50.out_ref = f32[8,128]{1,0:T(8,128)S(1)} custom-call(s32[8,4096]{1,0:T(8,128)} %panel_ref.1, f32[1,8]{1,0:T(1,128)} %bitcast.2, s32[2,8]{1,0:T(2,128)} %geno_ref.1), custom_call_target="tpu_custom_call" | custom-call | tf_op jit(solution)/shard_map/pallas_call | solution.py:589
  36.8 0.6 %shard_map.51 = (f32[2,8]{1,0:T(2,128)}, f32[1,2]{1,0:T(1,128)}) custom-call(f32[8,128]{1,0:T(8,128)S(1)} %shard_map.50.out_ref), custom_call_target="tpu_custom_call" | custom-call | tf_op jit(solution)/shard_map/pallas_call | solution.py:601

commit v8 on v7

--- a/solution.py
+++ b/solution.py
@@ -324,10 +324,10 @@
     out_ref,
     rate_own, geno_own, panel_own, panel_all, meta_all, tiles, emis, fwd, bwd,
     log_send, log_plane, log_mid, log_z, log_last,
-    solve_send, solve_recv, sum_send, sum_all, dose_send, dose_recv,
+    solve_send, solve_recv, sum_send, sum_all,
     load_sem, own_sem, tile_sem, known,
     panel_s, panel_r, meta_s, meta_r, plane_s, plane_r, z_s, z_r,
-    core_s, core_r, all_s, all_r, dose_s, dose_r,
+    core_s, core_r, all_s, all_r,
 ):
     n_group = BLOCKS
     n_x = n_group // 2
@@ -506,37 +506,36 @@
     total = (dot_nt(ones, coarse) + dot_nt(ones, fine))[0:1]
 
     everyone = [
-        (dx, dy, dz) for dx in range(n_x) for dy in range(n_y) for dz in range(n_z)
-        if dx or dy or dz
+        (dx, dy, dz, dc) for dx in range(n_x) for dy in range(n_y) for dz in range(n_z)
+        for dc in range(2) if dx or dy or dz or dc
     ]
     everyone.sort(
         key=lambda p: -(min(p[0], n_x - p[0]) + min(p[1], n_y - p[1]) + min(p[2], n_z - p[2]))
     )
     others = len(everyone)
+    half = (others + 1) // 2
     sum_send[...] = total
-    for i, (dx, dy, dz) in enumerate(everyone):
+    places = [1, half]
+    for dx, dy, dz, dc in everyone:
         peer = (
-            ((x + dx) % n_x) * 2 + core,
+            ((x + dx) % n_x) * 2 + (core + dc) % 2,
             ((z + dz) % n_z) * n_y + (y + dy) % n_y,
         )
-        remote(sum_send, sum_all.at[pl.ds(i, 1)], all_s, all_r, peer).start()
-    sum_all[others : others + 1] = total
+        remote(sum_send, sum_all.at[pl.ds(places[dc], 1)], all_s, all_r, peer).start()
+        places[dc] += 1
+    sum_all[0:1] = total
     swap.wait()
     other = solve_recv[...]
     out_ref[2:3, 0:2] = jnp.where(
         lane_row == 0, jnp.where(core == 0, like, other), jnp.where(core == 0, other, like)
     )[:, 0:2]
-    rest = pl.ds(0, others)
+    rest = pl.ds(1, others)
     remote(sum_all.at[rest], sum_all.at[rest], all_s, all_r, partner).wait()
-    total = jnp.sum(sum_all[...], axis=0, keepdims=True)
-    share = total / pltpu.roll(total, 64, 1)
-    dose_send[...] = share
-    trade = remote(dose_send, dose_recv, dose_s, dose_r, partner)
-    trade.start()
+    mine = jnp.sum(sum_all[0:half], axis=0, keepdims=True)
+    theirs = jnp.sum(sum_all[half:], axis=0, keepdims=True)
     shift = (128 - 8 * group) % 128
-    mine = pltpu.roll(share, shift, 1)
-    trade.wait()
-    theirs = pltpu.roll(dose_recv[...], shift, 1)
+    mine = pltpu.roll(mine / pltpu.roll(mine, 64, 1), shift, 1)
+    theirs = pltpu.roll(theirs / pltpu.roll(theirs, 64, 1), shift, 1)
     out_ref[0:1, 0:8] = jnp.where(core == 0, mine, theirs)[:, 0:8]
     out_ref[1:2, 0:8] = jnp.where(core == 0, theirs, mine)[:, 0:8]
 
@@ -574,9 +573,7 @@
         vmem((1, 128), F32),
         vmem((1, 128), F32),
         vmem((1, 128), F32),
-        vmem((n_group // 2 * n_batch, 128), F32),
-        vmem((1, 128), F32),
-        vmem((1, 128), F32),
+        vmem((n_group * n_batch, 128), F32),
         dma((3,)),
         dma,
         dma((8,)),
@@ -584,7 +581,7 @@
         dma, dma, dma, dma, dma, dma,
         dma, dma,
         dma, dma,
-        dma, dma, dma, dma,
+        dma, dma,
     ]
     out = pl.pallas_call(
         functools.partial(kernel, n_y, n_z, k),

time: 37.5 us -> 36.2 us (0.965)
  Pallas kernels: 36.8 us -> 35.4 us
    pallas_call x1, Pallas kernels: 36.2 us -> 34.9 us  [on_device(): pl.pallas_call(functools.partial(kernel, n_y, n_z, k), out_shape=pltpu.VM...]
where the time goes in v8:
time: 36.2 us; the launch traced here: 36.1 us
  Pallas kernels  35.4 us (98%)
  between operations  0.64 us (2%)
    pallas_call x1, Pallas kernels, on_device(): pl.pallas_call(functools.partial(kernel, n_y, n_z, k), out_shape=pltpu.VM...  34.9 us

profile of v8, /device:TPU:1, one launch (start us, length us, event | category | flops | bytes accessed | tf_op | source)
XLA Modules:
  0.0 36.1 jit_solution(521486349233636477)
XLA Ops:
  0.6 34.9 %shard_map.50.out_ref = f32[8,128]{1,0:T(8,128)S(1)} custom-call(s32[8,4096]{1,0:T(8,128)} %panel_ref.1, f32[1,8]{1,0:T(1,128)} %bitcast.2, s32[2,8]{1,0:T(2,128)} %geno_ref.1), custom_call_target="tpu_custom_call" | custom-call | tf_op jit(solution)/shard_map/pallas_call | solution.py:586
  35.5 0.6 %shard_map.51 = (f32[2,8]{1,0:T(2,128)}, f32[1,2]{1,0:T(1,128)}) custom-call(f32[8,128]{1,0:T(8,128)S(1)} %shard_map.50.out_ref), custom_call_target="tpu_custom_call" | custom-call | tf_op jit(solution)/shard_map/pallas_call | solution.py:598

commit v9 on v8

--- a/solution.py
+++ b/solution.py
@@ -333,28 +333,33 @@
     n_x = n_group // 2
     group = lax.axis_index("group")
     batch = lax.axis_index("batch")
-    core = group % 2
-    x = group // 2
-    y = batch % n_y
-    z = batch // n_y
-    partner = (group + 1 - 2 * core, batch)
+    x = lax.div(group, 2)
+    core = group - 2 * x
+    z = lax.div(batch, n_y)
+    y = batch - n_y * z
+    others_core = 1 - core
+    partner = (2 * x + others_core, batch)
     width = panel_all.shape[2]
     log_k = math.log(k)
+    first_of = [2 * lax.rem(x + d, n_x) for d in range(n_x)]
+    groups = [[first + core, first + others_core] for first in first_of]
+    ys = [lax.rem(y + d, n_y) for d in range(n_y)]
+    zs = [n_y * lax.rem(z + d, n_z) for d in range(n_z)]
 
     def in_group(d):
-        return (group + d) % n_group
+        return lax.rem(group + d, n_group)
 
     def group_peer(d):
         return (in_group(d), batch)
 
     def y_peer(d):
-        return (group, z * n_y + (y + d) % n_y)
+        return (group, n_y * z + ys[d])
 
     def z_peer(d):
-        return (group, ((z + d) % n_z) * n_y + y)
+        return (group, zs[d] + y)
 
     def plane_peer(dx, dy):
-        return (((x + dx) % n_x) * 2 + core, z * n_y + (y + dy) % n_y)
+        return (groups[dx][0], n_y * z + ys[dy])
 
     def remote(src, dst, send, recv, peer):
         return pltpu.make_async_remote_copy(
@@ -384,20 +389,20 @@
     )
     for load in loads:
         load.start()
-    own.start()
     barrier = pltpu.get_barrier_semaphore()
     near_y = [y_peer(d) for d in sorted({1, n_y - 1}) if 0 < d < n_y]
     near_z = [z_peer(d) for d in sorted({1, n_z - 1}) if 0 < d < n_z]
     peers = [group_peer(d) for d in far_first(n_group)] + near_y + near_z
     for peer in peers:
         pl.semaphore_signal(barrier, inc=1, device_id=peer, device_id_type=MESH)
+    own.start()
     finish(loads)
     meta_all[group] = meta_tile(rate_own[...], geno_own[...])
     pl.semaphore_wait(barrier, len(peers))
 
     copies = []
     for d in far_first(n_group):
-        start = pl.multiple_of(in_group(d) // 2 * width, width)
+        start = pl.multiple_of(lax.div(in_group(d), 2) * width, width)
         copies.append(
             remote(
                 panel_own.at[:, pl.ds(start, width)], panel_all.at[group],
@@ -421,14 +426,6 @@
     remote(meta_all.at[most], meta_all.at[most], meta_s, meta_r, partner).wait()
     remote(panel_all.at[most], panel_all.at[most], panel_s, panel_r, partner).wait()
 
-    relayout = []
-    for c in range(8):
-        copy = pltpu.make_async_copy(
-            panel_all.at[:, :, pl.ds(128 * c, 128)], tiles.at[:, :, c], tile_sem.at[c]
-        )
-        copy.start()
-        relayout.append(copy)
-
     meta = meta_all[...].reshape(MARKERS, 128)
     signs = 2.0 * panel_all[...].reshape(MARKERS, width).astype(F32) - 1.0
     genotype = jnp.where(core == 0, meta[:, 1:2], meta[:, 2:3])
@@ -445,6 +442,14 @@
     ]
     for copy in flying:
         copy.start()
+    relayout = []
+    for c in range(8):
+        copy = pltpu.make_async_copy(
+            panel_all.at[:, :, pl.ds(128 * c, 128)], tiles.at[:, :, c], tile_sem.at[c]
+        )
+        copy.start()
+        relayout.append(copy)
+
     rates = [meta[8 * a : 8 * a + 8, 0:1] for a in range(BLOCKS)]
     terms = rate_terms(rates, log_k)
     rate_row = row_of(rates)
@@ -470,6 +475,7 @@
         remote(log_z, log_z, z_s, z_r, partner).wait()
     log_last[0:20] = log_total([total] + [log_z[d] for d in range(n_z - 1)])
 
+    sum_send[...] = jnp.zeros((1, 128), F32)
     solved = solve(log_last[...], terms, log_k)
 
     lane_row = iota((1, 128), 1)
@@ -493,17 +499,17 @@
         behind = (keep_b[:, t : t + 1] * emis[t]) * behind + jump_b[:, t : t + 1]
 
     over_k = []
-    for which in range(2):
-        for a in range(BLOCKS):
-            both = fwd[8 * a : 8 * a + 8] * bwd[8 * a : 8 * a + 8]
-            if which == 0:
-                both = both * tiles[a].astype(F32)
-            over_k.append(gather_sublanes([both[i] for i in range(8)]))
+    for a in range(BLOCKS):
+        both = fwd[8 * a : 8 * a + 8] * bwd[8 * a : 8 * a + 8] * tiles[a].astype(F32)
+        over_k.append(gather_sublanes([both[i] for i in range(8)]))
     stacked = jnp.concatenate(over_k, axis=0)
     ones = jnp.ones((8, 128), BF16)
     coarse = stacked.astype(BF16)
     fine = (stacked - coarse.astype(F32)).astype(BF16)
     total = (dot_nt(ones, coarse) + dot_nt(ones, fine))[0:1]
+    after = jnp.where(lane_row == 127, 0.0, pltpu.roll(solved, 127, 1))
+    inverse = jnp.exp(solved + pltpu.roll(after, 64, 1) - (solved[:, 63:64] - log_k))
+    total = total * inverse[:, 0:64]
 
     everyone = [
         (dx, dy, dz, dc) for dx in range(n_x) for dy in range(n_y) for dz in range(n_z)
@@ -514,16 +520,14 @@
     )
     others = len(everyone)
     half = (others + 1) // 2
-    sum_send[...] = total
+    sum_send[:, 0:64] = total
     places = [1, half]
     for dx, dy, dz, dc in everyone:
-        peer = (
-            ((x + dx) % n_x) * 2 + (core + dc) % 2,
-            ((z + dz) % n_z) * n_y + (y + dy) % n_y,
-        )
+        peer = (groups[dx][dc], zs[dz] + ys[dy])
         remote(sum_send, sum_all.at[pl.ds(places[dc], 1)], all_s, all_r, peer).start()
         places[dc] += 1
-    sum_all[0:1] = total
+    sum_all[0:1, 0:64] = total
+    sum_all[0:1, 64:128] = jnp.zeros((1, 64), F32)
     swap.wait()
     other = solve_recv[...]
     out_ref[2:3, 0:2] = jnp.where(
@@ -533,9 +537,9 @@
     remote(sum_all.at[rest], sum_all.at[rest], all_s, all_r, partner).wait()
     mine = jnp.sum(sum_all[0:half], axis=0, keepdims=True)
     theirs = jnp.sum(sum_all[half:], axis=0, keepdims=True)
-    shift = (128 - 8 * group) % 128
-    mine = pltpu.roll(mine / pltpu.roll(mine, 64, 1), shift, 1)
-    theirs = pltpu.roll(theirs / pltpu.roll(theirs, 64, 1), shift, 1)
+    shift = lax.rem(128 - 8 * group, 128)
+    mine = pltpu.roll(mine, shift, 1)
+    theirs = pltpu.roll(theirs, shift, 1)
     out_ref[0:1, 0:8] = jnp.where(core == 0, mine, theirs)[:, 0:8]
     out_ref[1:2, 0:8] = jnp.where(core == 0, theirs, mine)[:, 0:8]
 

time: 36.2 us -> 35.9 us (level)
  no operation moved by 1% of the time
where the time goes in v9:
time: 35.9 us; the launch traced here: 35.8 us
  Pallas kernels  35.1 us (98%)
  between operations  0.64 us (2%)
    pallas_call x1, Pallas kernels, on_device(): pl.pallas_call(functools.partial(kernel, n_y, n_z, k), out_shape=pltpu.VM...  34.6 us

profile of v9, /device:TPU:1, one launch (start us, length us, event | category | flops | bytes accessed | tf_op | source)
XLA Modules:
  0.0 35.8 jit_solution(6087186341079677611)
XLA Ops:
  0.6 34.6 %shard_map.50.out_ref = f32[8,128]{1,0:T(8,128)S(1)} custom-call(s32[8,4096]{1,0:T(8,128)} %panel_ref.1, f32[1,8]{1,0:T(1,128)} %bitcast.2, s32[2,8]{1,0:T(2,128)} %geno_ref.1), custom_call_target="tpu_custom_call" | custom-call | tf_op jit(solution)/shard_map/pallas_call | solution.py:590
  35.2 0.6 %shard_map.51 = (f32[2,8]{1,0:T(2,128)}, f32[1,2]{1,0:T(1,128)}) custom-call(f32[8,128]{1,0:T(8,128)S(1)} %shard_map.50.out_ref), custom_call_target="tpu_custom_call" | custom-call | tf_op jit(solution)/shard_map/pallas_call | solution.py:602

commit v10 on v9

--- a/solution.py
+++ b/solution.py
@@ -516,7 +516,10 @@
         for dc in range(2) if dx or dy or dz or dc
     ]
     everyone.sort(
-        key=lambda p: -(min(p[0], n_x - p[0]) + min(p[1], n_y - p[1]) + min(p[2], n_z - p[2]))
+        key=lambda p: (
+            -min(p[2], n_z - p[2]),
+            -(min(p[0], n_x - p[0]) + min(p[1], n_y - p[1])),
+        )
     )
     others = len(everyone)
     half = (others + 1) // 2

time: 35.9 us -> 35.9 us (level)
  no operation moved by 1% of the time
where the time goes in v10:
time: 35.9 us; the launch traced here: 35.8 us
  Pallas kernels  35.1 us (98%)
  between operations  0.64 us (2%)
    pallas_call x1, Pallas kernels, on_device(): pl.pallas_call(functools.partial(kernel, n_y, n_z, k), out_shape=pltpu.VM...  34.6 us

profile of v10, /device:TPU:1, one launch (start us, length us, event | category | flops | bytes accessed | tf_op | source)
XLA Modules:
  0.0 35.8 jit_solution(16254130647059696616)
XLA Ops:
  0.6 34.6 %shard_map.50.out_ref = f32[8,128]{1,0:T(8,128)S(1)} custom-call(s32[8,4096]{1,0:T(8,128)} %panel_ref.1, f32[1,8]{1,0:T(1,128)} %bitcast.2, s32[2,8]{1,0:T(2,128)} %geno_ref.1), custom_call_target="tpu_custom_call" | custom-call | tf_op jit(solution)/shard_map/pallas_call | solution.py:593
  35.2 0.6 %shard_map.51 = (f32[2,8]{1,0:T(2,128)}, f32[1,2]{1,0:T(1,128)}) custom-call(f32[8,128]{1,0:T(8,128)S(1)} %shard_map.50.out_ref), custom_call_target="tpu_custom_call" | custom-call | tf_op jit(solution)/shard_map/pallas_call | solution.py:605
